TPU v7x, 32 devices: a whole 2x2x4 slice. The times are simulated.
32 devices in a mesh: member: 2 (over x), fsdp: 16 (over z, y, core).
Axes of the slice: x: 2, y: 2, z: 4, core: 2. Of those that a mesh axis runs over, the one named last changes fastest.
Arguments:
- context: bfloat16 [4, 2048, 2048], P(None, 'fsdp', 'member'), may hold values from -6 to 6
- residual: bfloat16 [2048, 2048], P('fsdp', 'member'), may hold values from -6 to 6
- out_weight: bfloat16 [2048, 2048], P('fsdp', 'member'), may hold values from -0.1875 to 0.1875
- in_factor: bfloat16 [4, 2048], P(None, 'member'), may hold values from 0.25 to 1.75
- out_factor: bfloat16 [4, 2048], P(None, 'member'), may hold values from 0.25 to 1.75
- cotangent: bfloat16 [4, 2048, 2048], P(None, 'fsdp', 'member'), may hold values from -0.796875 to 0.796875
Outputs:
- hidden: bfloat16 [4, 2048, 2048], P(None, 'fsdp', 'member')
- grad_context: bfloat16 [4, 2048, 2048], P(None, 'fsdp', 'member')
- grad_weight: float32 [2048, 2048], P('fsdp', 'member')
- grad_in_factor: float32 [4, 2048], P(None, 'member')
- grad_out_factor: float32 [4, 2048], P(None, 'member')
- grad_residual: float32 [2048, 2048], P('fsdp', 'member')
All inputs are finite; a program needn't handle non-finite values.
Results may differ from a plain program's by a relative error of at most 0.013.
Values may be sent and summed in bfloat16 or wider, within the bound.
A program may use at most 64 MiB of HBM per device.

v0:
```python
import functools

import jax
import jax.numpy as jnp
from jax import lax
from jax.experimental import pallas as pl
from jax.experimental.pallas import tpu as pltpu
from jax.sharding import PartitionSpec as P

F32 = jnp.float32
BF16 = jnp.bfloat16


def general(context, residual, out_weight, in_factor, out_factor, cotangent):
    in_wide = in_factor.astype(jnp.float32)
    out_wide = out_factor.astype(jnp.float32)
    scaled_local = (context.astype(jnp.float32) * in_wide[:, None, :]).astype(jnp.bfloat16)
    scaled_grad = (cotangent.astype(jnp.float32) * out_wide[:, None, :]).astype(jnp.bfloat16)
    scaled_context = lax.all_gather(scaled_local, "member", axis=2, tiled=True)
    weight = lax.all_gather(out_weight, "fsdp", axis=0, tiled=True)
    projected = jnp.einsum(
        "eti,id->etd", scaled_context, weight, preferred_element_type=jnp.float32
    )
    partial_value = jnp.einsum(
        "etd,id->eti", scaled_grad, weight, preferred_element_type=jnp.float32
    )
    hidden = (residual.astype(jnp.float32)[None] + projected * out_wide[:, None, :]).astype(
        jnp.bfloat16
    )
    backward = lax.psum_scatter(
        partial_value.astype(jnp.bfloat16), "member", scatter_dimension=2, tiled=True
    ).astype(jnp.float32)
    grad_context = (backward * in_wide[:, None, :]).astype(jnp.bfloat16)
    grad_in_local = jnp.sum(context.astype(jnp.float32) * backward, axis=1)
    grad_out_local = jnp.sum(cotangent.astype(jnp.float32) * projected, axis=1)
    grad_in, grad_out = lax.psum((grad_in_local, grad_out_local), "fsdp")
    grad_block = jnp.einsum(
        "eti,etd->id", scaled_context, scaled_grad, preferred_element_type=jnp.float32
    )
    grad_weight = lax.psum_scatter(grad_block, "fsdp", scatter_dimension=0, tiled=True)
    grad_residual = jnp.sum(cotangent.astype(jnp.float32), axis=0)
    return (hidden, grad_context, grad_weight, grad_in, grad_out, grad_residual)


def kernel(
    C,
    ctx_h, res, w_h, inf, outf, cot_h,
    hid, gc, gw, gi, go, gr,
    ctx, cot, cbuf, infx, sc, sg, wb, proj, part, xrecv, gall, psend, precv, rsend, rrecv, arb, arr, swp,
    ld_sem, cx_ss, cx_rs, ag_ss, ag_rs, pt_ss, pt_rs, px_ss, px_rs, ps_ss, ps_rs, rs_ss, rs_rs, ar_ss, ar_rs,
):
    E, T, H = ctx.shape
    M = E * T
    R = w_h.shape[0]
    R2 = 2 * R
    S = R // 2
    half = C // 2
    far = C // 2
    bits = []
    b = 1
    while b < 2 * C:
        bits.append(b)
        b *= 2

    m = lax.axis_index("member")
    f = lax.axis_index("fsdp")
    c = f % 2
    q = f // 2
    p = (1 - q % 2) * (q // 2) + (q % 2) * (C - 1 - q // 2)

    def chip_at(offset):
        pos = (p + offset + C) % C
        y = pos // half
        return 2 * ((1 - y) * pos + y * (C - 1 - pos)) + y

    peer = (1 - m, f)
    partner = (m, q * 2 + 1 - c)
    nxt = (m, chip_at(1) * 2 + c)
    prv = (m, chip_at(-1) * 2 + c)
    side = (nxt, prv)
    sign = (1, -1)
    flips = [(m, f + bit * (1 - 2 * ((f // bit) % 2))) for bit in bits]

    def rc(src, dst, ss, rs, dev):
        return pltpu.make_async_remote_copy(
            src_ref=src, dst_ref=dst, send_sem=ss, recv_sem=rs,
            device_id=dev, device_id_type=pl.DeviceIdType.MESH,
        )

    barrier = pltpu.get_barrier_semaphore()
    greet = [peer, nxt, prv] + flips
    for dev in greet:
        pl.semaphore_signal(barrier, inc=1, device_id=dev, device_id_type=pl.DeviceIdType.MESH)

    def rows_of(core):
        return pl.ds(pl.multiple_of(core * R, R), R)

    ld_ctx = pltpu.make_async_copy(ctx_h, ctx, ld_sem.at[0])
    ld_cot = pltpu.make_async_copy(cot_h, cot, ld_sem.at[1])
    ld_w = pltpu.make_async_copy(w_h, wb.at[q, rows_of(c)], ld_sem.at[2])
    ld_ctx.start()
    ld_cot.start()
    ld_w.start()

    inw = inf[...].astype(F32)
    outw = outf[...].astype(F32)

    def cx(e):
        return rc(ctx_h.at[:, :, pl.ds(e * R2, R2)], cbuf.at[e], cx_ss.at[e], cx_rs.at[e], peer)

    cxf = rc(inf, infx, cx_ss.at[half], cx_rs.at[half], peer)

    def sub(core, u):
        return pl.ds(pl.multiple_of(core * R + u * S, S), S)

    def subs(d, s):
        return (0, 1) if s < far else (d,)

    def ag(d, s, u, shift):
        qq = chip_at(-sign[d] * (s - 1 + shift))
        dst = wb.at[qq, sub(c, u)]
        src = w_h.at[pl.ds(u * S, S)] if (s == 1 and shift == 0) else dst
        return rc(src, dst, ag_ss.at[d, s - 1, u], ag_rs.at[d, s - 1, u], side[d])

    def pt(k, u, offset, mine):
        qq = chip_at(offset)
        dst = wb.at[qq, sub(c if mine else 1 - c, u)]
        src = w_h.at[pl.ds(u * S, S)] if (mine and k == 0) else dst
        return rc(src, dst, pt_ss.at[k, u], pt_rs.at[k, u], partner)

    sends = []

    def go_send(copy):
        copy.start()
        sends.append(copy)

    pl.semaphore_wait(barrier, len(greet))
    go_send(cxf)
    for j in range(half):
        go_send(cx(j))
    for u in range(2):
        for d in range(2):
            go_send(ag(d, 1, u, 0))
        go_send(pt(0, u, 0, True))

    ld_ctx.wait()
    for e in range(E):
        v = (ctx[e].astype(F32) * inw[e:e + 1]).astype(BF16)
        for j in range(half):
            sc[m * half + j, e * T:(e + 1) * T, :] = v[:, j * R2:(j + 1) * R2]
    ld_cot.wait()
    for e in range(E):
        sg[e * T:(e + 1) * T, :] = (cot[e].astype(F32) * outw[e:e + 1]).astype(BF16)
    proj[...] = jnp.zeros(proj.shape, F32)

    def px(qq):
        return rc(part.at[qq], xrecv.at[qq % half], px_ss.at[qq % half], px_rs.at[qq % half], peer)

    def ps(qq):
        return rc(psend.at[qq], precv.at[qq], ps_ss.at[qq], ps_rs.at[qq], partner)

    def gw_one(qq):
        g = lax.dot_general(sc[qq], sg[...], (((0,), (0,)), ((), ())), preferred_element_type=F32)
        gall[qq, 0] = g[:R]
        gall[qq, 1] = g[R:]
        psend[qq] = gall[qq, 1 - c].astype(BF16)
        ps(qq).start()

    def gw_half(h):
        def body(j, carry):
            gw_one(h * half + j)
            return carry
        lax.fori_loop(0, half, body, 0)

    def project(qq):
        proj[...] += jnp.dot(sc[qq], wb[qq], preferred_element_type=F32)

    def process(offsets):
        def body(j, carry):
            off = offsets[0] if len(offsets) == 1 else offsets[0] + j * (offsets[1] - offsets[0])
            qq = chip_at(off)
            part[qq] = lax.dot_general(
                sg[...], wb[qq], (((1,), (1,)), ((), ())), preferred_element_type=F32
            ).astype(BF16)

            @pl.when(qq // half != m)
            def _():
                px(qq).start()

            @pl.when(qq // half == m)
            def _():
                project(qq)
            return carry
        lax.fori_loop(0, len(offsets), body, 0)

    def rs(d, k, u):
        rows = pl.ds(u * S, S)
        return rc(rsend.at[d, k, rows], rrecv.at[d, k, rows], rs_ss.at[d, k, u], rs_rs.at[d, k, u], side[d])

    def chip_sum(qq, u):
        rows = slice(u * S, (u + 1) * S)
        return gall[qq, c, rows, :] + precv[qq, rows, :].astype(F32)

    def rs_step(k):
        if k == 0:
            qf = chip_at(far)
            ps(qf).wait_recv()
            for d in range(2):
                rsend[d, 0, d * S:(d + 1) * S, :] = chip_sum(qf, d).astype(BF16)
                go_send(rs(d, 0, d))
            return
        qs = [chip_at(sign[d] * (far - k)) for d in range(2)]
        for d in range(2):
            ps(qs[d]).wait_recv()
        for i in range(2):
            for d in range(2):
                u = (1 - d if i == 0 else d) if k == 1 else i
                rows = slice(u * S, (u + 1) * S)
                v = chip_sum(qs[d], u)
                if k > 1 or u == d:
                    rs(d, k - 1, u).wait_recv()
                    v = v + rrecv[d, k - 1, rows, :].astype(F32)
                rsend[d, k, rows, :] = v.astype(BF16)
                go_send(rs(d, k, u))

    gw_half(m)
    ld_w.wait()
    for u in range(2):
        pt(0, u, 0, False).wait_recv()
    process([0])
    cxf_in = cxf

    def scale_in(j):
        cx(j).wait_recv()
        for e in range(E):
            wide = infx[e:e + 1, j * R2:(j + 1) * R2].astype(F32)
            sc[(1 - m) * half + j, e * T:(e + 1) * T, :] = (cbuf[j, e].astype(F32) * wide).astype(BF16)
        gw_one((1 - m) * half + j)

    for s in range(1, far):
        for u in range(2):
            for d in range(2):
                ag(d, s, u, 1).wait_recv()
                if u in subs(d, s + 1):
                    go_send(ag(d, s + 1, u, 0))
                go_send(pt(d * (far - 1) + s, u, -sign[d] * s, True))
        if s == 1:
            gr[...] = jnp.sum(cot[...].astype(F32), axis=0)
        for u in range(2):
            for d in range(2):
                pt(d * (far - 1) + s, u, -sign[d] * s, False).wait_recv()
        process([-s, s])
        if s == 1:
            cxf_in.wait_recv()
        if s >= 2:
            scale_in(s - 2)
    for d in range(2):
        ag(d, far, d, 1).wait_recv()
        go_send(pt(2 * far - 1, d, far, True))
    for d in range(2):
        pt(2 * far - 1, d, far, False).wait_recv()
    process([far])
    for j in range(far - 2, half):
        scale_in(j)
    rs_step(0)

    def project_rest(lo, hi):
        def body(j, carry):
            project((1 - m) * half + j)
            return carry
        lax.fori_loop(lo, hi, body, 0)

    project_rest(0, half)
    rs_step(1)
    resw = res[...].astype(F32)
    for e in range(E):
        pe = proj[e * T:(e + 1) * T, :]
        hid[e] = (resw + pe * outw[e:e + 1]).astype(BF16)
        arb[0, 2 * E + e:2 * E + e + 1, :] = jnp.sum(cot[e].astype(F32) * pe, axis=0, keepdims=True)
    for j in range(half):
        cols = slice(j * R2, (j + 1) * R2)
        for e in range(E):
            rows = slice(e * T, (e + 1) * T)
            a = ctx[e, :, cols].astype(F32) * part[m * half + j, rows, :].astype(F32)
            arb[0, e:e + 1, cols] = jnp.sum(a, axis=0, keepdims=True)
            a = cbuf[j, e].astype(F32) * part[(1 - m) * half + j, rows, :].astype(F32)
            arb[0, E + e:E + e + 1, cols] = jnp.sum(a, axis=0, keepdims=True)

    def ar(i):
        return rc(arb.at[i], arr.at[i], ar_ss.at[i], ar_rs.at[i], flips[i])

    swap = rc(swp.at[0], swp.at[1], cx_ss.at[half + 1], cx_rs.at[half + 1], peer)

    def ar_step(i):
        ar(i).wait_recv()
        total = arb[i] + arr[i]
        if i + 1 < len(bits):
            arb[i + 1] = total
            go_send(ar(i + 1))
        else:
            swp[0] = total[E:2 * E]
            go_send(swap)
            gi[...] = total[:E]
            go[...] = total[2 * E:]

    go_send(ar(0))
    ar_step(0)
    done = 1
    for k in range(2, far):
        rs_step(k)
        if done < len(bits):
            ar_step(done)
            done += 1
    while done < len(bits):
        ar_step(done)
        done += 1

    ps(q).wait_recv()
    for u in range(2):
        rows = slice(u * S, (u + 1) * S)
        own = chip_sum(q, u)
        for d in range(2):
            rs(d, far - 1, u).wait_recv()
            own = own + rrecv[d, far - 1, rows, :].astype(F32)
        gw[rows, :] = own

    for j in range(half):
        rc(xrecv.at[j], xrecv.at[j], px_ss.at[j], px_rs.at[j], peer).wait_recv()
        cols = slice(j * R2, (j + 1) * R2)
        for e in range(E):
            rows = slice(e * T, (e + 1) * T)
            be = part[m * half + j, rows, :].astype(F32) + xrecv[j, rows, :].astype(F32)
            gc[e, :, cols] = (be * inw[e:e + 1, cols]).astype(BF16)

    swap.wait_recv()
    gi[...] += swp[1]

    for copy in sends:
        copy.wait_send()

    def drain(j, carry):
        ps(j).wait_send()
        return carry
    lax.fori_loop(0, C, drain, 0)
    for j in range(half):
        rc(part.at[(1 - m) * half + j], xrecv.at[j], px_ss.at[j], px_rs.at[j], peer).wait_send()


def fused(C, context, residual, out_weight, in_factor, out_factor, cotangent):
    E, T, H = context.shape
    M = E * T
    R = out_weight.shape[0]
    half = C // 2
    far = half
    steps = (2 * C).bit_length() - 1
    vm = pl.BlockSpec(memory_space=pltpu.VMEM)
    hbm = pl.BlockSpec(memory_space=pl.ANY)
    dma = pltpu.SemaphoreType.DMA
    shape = jax.ShapeDtypeStruct
    results = pl.pallas_call(
        functools.partial(kernel, C),
        out_shape=(
            shape((E, T, H), BF16),
            shape((E, T, H), BF16),
            shape((R, H), F32),
            shape((E, H), F32),
            shape((E, H), F32),
            shape((T, H), F32),
        ),
        in_specs=[hbm, vm, hbm, vm, vm, hbm],
        out_specs=tuple([vm] * 6),
        scratch_shapes=[
            pltpu.VMEM((E, T, H), BF16),
            pltpu.VMEM((E, T, H), BF16),
            pltpu.VMEM((half, E, T, 2 * R), BF16),
            pltpu.VMEM((E, H), BF16),
            pltpu.VMEM((C, M, 2 * R), BF16),
            pltpu.VMEM((M, H), BF16),
            pltpu.VMEM((C, 2 * R, H), BF16),
            pltpu.VMEM((M, H), F32),
            pltpu.VMEM((C, M, 2 * R), BF16),
            pltpu.VMEM((half, M, 2 * R), BF16),
            pltpu.VMEM((C, 2, R, H), F32),
            pltpu.VMEM((C, R, H), BF16),
            pltpu.VMEM((C, R, H), BF16),
            pltpu.VMEM((2, far, R, H), BF16),
            pltpu.VMEM((2, far, R, H), BF16),
            pltpu.VMEM((steps, 3 * E, H), F32),
            pltpu.VMEM((steps, 3 * E, H), F32),
            pltpu.VMEM((2, E, H), F32),
            dma((3,)),
            dma((half + 2,)),
            dma((half + 2,)),
            dma((2, far, 2)),
            dma((2, far, 2)),
            dma((2 * far, 2)),
            dma((2 * far, 2)),
            dma((half,)),
            dma((half,)),
            dma((C,)),
            dma((C,)),
            dma((2, far, 2)),
            dma((2, far, 2)),
            dma((steps,)),
            dma((steps,)),
        ],
        compiler_params=pltpu.CompilerParams(
            collective_id=0, has_side_effects=True, vmem_limit_bytes=60 * 1024 * 1024
        ),
    )(context, residual, out_weight, in_factor, out_factor, cotangent)
    return pl.pallas_call(
        deliver,
        out_shape=tuple(shape(r.shape, r.dtype) for r in results),
        in_specs=[hbm] * 6,
        out_specs=tuple([hbm] * 6),
        scratch_shapes=[pltpu.VMEM(r.shape, r.dtype) for r in results] + [dma((2, 6))],
    )(*results)


def deliver(*refs):
    sources, results, held, sem = refs[:6], refs[6:12], refs[12:18], refs[18]
    loads = [pltpu.make_async_copy(sources[i], held[i], sem.at[0, i]) for i in range(6)]
    stores = [pltpu.make_async_copy(held[i], results[i], sem.at[1, i]) for i in range(6)]
    for copy in loads:
        copy.start()
    for i in range(6):
        loads[i].wait()
        stores[i].start()
    for copy in stores:
        copy.wait()


def solution(mesh):
    in_specs = (
        P(None, "fsdp", "member"),
        P("fsdp", "member"),
        P("fsdp", "member"),
        P(None, "member"),
        P(None, "member"),
        P(None, "fsdp", "member"),
    )
    out_specs = (
        P(None, "fsdp", "member"),
        P(None, "fsdp", "member"),
        P("fsdp", "member"),
        P(None, "member"),
        P(None, "member"),
        P("fsdp", "member"),
    )
    members = mesh.shape["member"]
    chips = mesh.shape["fsdp"] // 2
    if members == 2 and chips >= 8 and chips & (chips - 1) == 0:
        per_device = functools.partial(fused, chips)
    else:
        per_device = general
    return jax.shard_map(
        per_device, mesh=mesh, in_specs=in_specs, out_specs=out_specs, check_vma=False
    )
```

profile of v0, /device:TPU:0, one launch (start us, length us, event | category | flops | bytes accessed | tf_op | source)
XLA Modules:
  0.0 67.2 jit_solution(4535669734346557222)
XLA Ops:
  0.6 63.5 %shard_map.109 = (bf16[4,128,1024]{2,1,0:T(8,128)(2,1)}, bf16[4,128,1024]{2,1,0:T(8,128)(2,1)}, f32[128,1024]{1,0:T(8,128)}, f32[4,1024]{1,0:T(4,128)}, f32[4,1024]{1,0:T(4,128)}, /*index=5*/f32[128,1024]{1,0:T(8,128)}) custom-call(bf16[4,128,1024]{2,1,0:T(8,128)(2,1)} %ctx_h.1, bf16[128,1024]{1,0:T(8,128)(2,1)} %res.1, bf16[128,1024]{1,0:T(8,128)(2,1)} %w_h.1, ...), custom_call_target="tpu_custom_call" | custom-call | tf_op jit(solution)/shard_map/pallas_call | solution.py:360
  64.2 3.0 %shard_map.110 = (bf16[4,128,1024]{2,1,0:T(8,128)(2,1)}, bf16[4,128,1024]{2,1,0:T(8,128)(2,1)}, f32[128,1024]{1,0:T(8,128)}, f32[4,1024]{1,0:T(4,128)}, f32[4,1024]{1,0:T(4,128)}, /*index=5*/f32[128,1024]{1,0:T(8,128)}) custom-call(bf16[4,128,1024]{2,1,0:T(8,128)(2,1)} %get-tuple-element.12.refs_0_, bf16[4,128,1024]{2,1,0:T(8,128)(2,1)} %get-tuple-element.13.refs_1_, ...), custom_call_target="tpu_custom_call" | custom-call | tf_op jit(solution)/shard_map/pallas_call | solution.py:411
where the time goes:
time: 67.3 us; the launch traced here: 67.2 us
  Pallas kernels  66.5 us (99%)
    pallas_call x1, Pallas kernels, fused(): pl.pallas_call(functools.partial(kernel, C), out_shape=(shape((E, T, H),...  63.5 us
    pallas_call x1, Pallas kernels, fused(): pl.pallas_call(deliver, out_shape=tuple((shape(r.shape, r.dtype) for r in...  3 us

commit v1 on v0

--- a/solution.py
+++ b/solution.py
@@ -44,13 +44,12 @@
 
 def kernel(
     C,
-    ctx_h, res, w_h, inf, outf, cot_h,
+    ctx_h, res_h, w_h, inf_h, outf_h, cot_h,
     hid, gc, gw, gi, go, gr,
-    ctx, cot, cbuf, infx, sc, sg, wb, proj, part, xrecv, gall, psend, precv, rsend, rrecv, arb, arr, swp,
+    ctx, cot, res, inf, outf, cbuf, infx, sc, sg, wb, proj, part, xrecv, gall, psend, precv, rsend, rrecv, arb, arr, swp,
     ld_sem, cx_ss, cx_rs, ag_ss, ag_rs, pt_ss, pt_rs, px_ss, px_rs, ps_ss, ps_rs, rs_ss, rs_rs, ar_ss, ar_rs,
 ):
     E, T, H = ctx.shape
-    M = E * T
     R = w_h.shape[0]
     R2 = 2 * R
     S = R // 2
@@ -88,27 +87,47 @@
         )
 
     barrier = pltpu.get_barrier_semaphore()
-    greet = [peer, nxt, prv] + flips
+    greet = [peer, partner, nxt, prv]
     for dev in greet:
         pl.semaphore_signal(barrier, inc=1, device_id=dev, device_id_type=pl.DeviceIdType.MESH)
 
     def rows_of(core):
         return pl.ds(pl.multiple_of(core * R, R), R)
 
-    ld_ctx = pltpu.make_async_copy(ctx_h, ctx, ld_sem.at[0])
-    ld_cot = pltpu.make_async_copy(cot_h, cot, ld_sem.at[1])
-    ld_w = pltpu.make_async_copy(w_h, wb.at[q, rows_of(c)], ld_sem.at[2])
-    ld_ctx.start()
-    ld_cot.start()
-    ld_w.start()
-
-    inw = inf[...].astype(F32)
-    outw = outf[...].astype(F32)
-
-    def cx(e):
-        return rc(ctx_h.at[:, :, pl.ds(e * R2, R2)], cbuf.at[e], cx_ss.at[e], cx_rs.at[e], peer)
-
-    cxf = rc(inf, infx, cx_ss.at[half], cx_rs.at[half], peer)
+    def load(i, src, dst):
+        copy = pltpu.make_async_copy(src, dst, ld_sem.at[i])
+        copy.start()
+        return copy
+
+    ld_inf = load(0, inf_h, inf)
+    ld_ctx = load(1, ctx_h, ctx)
+    ld_outf = load(2, outf_h, outf)
+    ld_cot = load(3, cot_h, cot)
+    ld_w = load(4, w_h, wb.at[q, rows_of(c)])
+    ld_res = load(5, res_h, res)
+
+    order = [chip_at(-far)] + [chip_at(s * (far - k)) for k in range(1, far) for s in sign] + [q]
+
+    def ranked(side_of):
+        found = [0] * half
+        count = 0
+        for chip in order:
+            member = chip // half == side_of
+            for n in range(half):
+                found[n] = jnp.where(jnp.logical_and(member, count == n), chip, found[n])
+            count = count + jnp.where(member, 1, 0)
+        return found
+
+    mine = ranked(m)
+    theirs = ranked(1 - m)
+
+    def cols_of(chip):
+        return pl.ds(pl.multiple_of((chip % half) * R2, R2), R2)
+
+    def cx(n):
+        return rc(ctx_h.at[:, :, cols_of(mine[n])], cbuf.at[n], cx_ss.at[n], cx_rs.at[n], peer)
+
+    cxf = rc(inf_h, infx, cx_ss.at[half], cx_rs.at[half], peer)
 
     def sub(core, u):
         return pl.ds(pl.multiple_of(core * R + u * S, S), S)
@@ -122,10 +141,10 @@
         src = w_h.at[pl.ds(u * S, S)] if (s == 1 and shift == 0) else dst
         return rc(src, dst, ag_ss.at[d, s - 1, u], ag_rs.at[d, s - 1, u], side[d])
 
-    def pt(k, u, offset, mine):
+    def pt(k, u, offset, own):
         qq = chip_at(offset)
-        dst = wb.at[qq, sub(c if mine else 1 - c, u)]
-        src = w_h.at[pl.ds(u * S, S)] if (mine and k == 0) else dst
+        dst = wb.at[qq, sub(c if own else 1 - c, u)]
+        src = w_h.at[pl.ds(u * S, S)] if (own and k == 0) else dst
         return rc(src, dst, pt_ss.at[k, u], pt_rs.at[k, u], partner)
 
     sends = []
@@ -136,22 +155,25 @@
 
     pl.semaphore_wait(barrier, len(greet))
     go_send(cxf)
-    for j in range(half):
-        go_send(cx(j))
+    for n in range(half):
+        go_send(cx(n))
     for u in range(2):
         for d in range(2):
             go_send(ag(d, 1, u, 0))
         go_send(pt(0, u, 0, True))
 
+    ld_inf.wait()
     ld_ctx.wait()
+    inw = inf[...].astype(F32)
     for e in range(E):
         v = (ctx[e].astype(F32) * inw[e:e + 1]).astype(BF16)
         for j in range(half):
             sc[m * half + j, e * T:(e + 1) * T, :] = v[:, j * R2:(j + 1) * R2]
+    ld_outf.wait()
     ld_cot.wait()
+    outw = outf[...].astype(F32)
     for e in range(E):
         sg[e * T:(e + 1) * T, :] = (cot[e].astype(F32) * outw[e:e + 1]).astype(BF16)
-    proj[...] = jnp.zeros(proj.shape, F32)
 
     def px(qq):
         return rc(part.at[qq], xrecv.at[qq % half], px_ss.at[qq % half], px_rs.at[qq % half], peer)
@@ -166,11 +188,18 @@
         psend[qq] = gall[qq, 1 - c].astype(BF16)
         ps(qq).start()
 
-    def gw_half(h):
-        def body(j, carry):
-            gw_one(h * half + j)
+    def order_at(i):
+        return chip_at((far - (i + 1) // 2) * (1 - 2 * ((i + 1) % 2)))
+
+    def gw_mine():
+        def body(i, carry):
+            qq = order_at(i)
+
+            @pl.when(qq // half == m)
+            def _():
+                gw_one(qq)
             return carry
-        lax.fori_loop(0, half, body, 0)
+        lax.fori_loop(0, C, body, 0)
 
     def project(qq):
         proj[...] += jnp.dot(sc[qq], wb[qq], preferred_element_type=F32)
@@ -201,41 +230,35 @@
         rows = slice(u * S, (u + 1) * S)
         return gall[qq, c, rows, :] + precv[qq, rows, :].astype(F32)
 
-    def rs_step(k):
+    def rs_sub(k, late):
         if k == 0:
-            qf = chip_at(far)
-            ps(qf).wait_recv()
-            for d in range(2):
-                rsend[d, 0, d * S:(d + 1) * S, :] = chip_sum(qf, d).astype(BF16)
-                go_send(rs(d, 0, d))
-            return
-        qs = [chip_at(sign[d] * (far - k)) for d in range(2)]
+            ps(chip_at(-far)).wait_recv()
         for d in range(2):
-            ps(qs[d]).wait_recv()
-        for i in range(2):
-            for d in range(2):
-                u = (1 - d if i == 0 else d) if k == 1 else i
-                rows = slice(u * S, (u + 1) * S)
-                v = chip_sum(qs[d], u)
-                if k > 1 or u == d:
-                    rs(d, k - 1, u).wait_recv()
-                    v = v + rrecv[d, k - 1, rows, :].astype(F32)
-                rsend[d, k, rows, :] = v.astype(BF16)
-                go_send(rs(d, k, u))
-
-    gw_half(m)
+            qq = chip_at(sign[d] * (far - k)) if k else chip_at(-far)
+            if k and not late:
+                ps(qq).wait_recv()
+            u = d if late else 1 - d
+            rows = slice(u * S, (u + 1) * S)
+            v = chip_sum(qq, u)
+            if k > 1 or (k == 1 and late):
+                rs(d, k - 1, u).wait_recv()
+                v = v + rrecv[d, k - 1, rows, :].astype(F32)
+            rsend[d, k, rows, :] = v.astype(BF16)
+            go_send(rs(d, k, u))
+
+    proj[...] = jnp.zeros(proj.shape, F32)
+    gw_mine()
     ld_w.wait()
     for u in range(2):
         pt(0, u, 0, False).wait_recv()
     process([0])
-    cxf_in = cxf
-
-    def scale_in(j):
-        cx(j).wait_recv()
+
+    def scale_in(n):
+        cx(n).wait_recv()
         for e in range(E):
-            wide = infx[e:e + 1, j * R2:(j + 1) * R2].astype(F32)
-            sc[(1 - m) * half + j, e * T:(e + 1) * T, :] = (cbuf[j, e].astype(F32) * wide).astype(BF16)
-        gw_one((1 - m) * half + j)
+            wide = infx[e:e + 1, cols_of(theirs[n])].astype(F32)
+            sc[theirs[n], e * T:(e + 1) * T, :] = (cbuf[n, e].astype(F32) * wide).astype(BF16)
+        gw_one(theirs[n])
 
     for s in range(1, far):
         for u in range(2):
@@ -244,6 +267,8 @@
                 if u in subs(d, s + 1):
                     go_send(ag(d, s + 1, u, 0))
                 go_send(pt(d * (far - 1) + s, u, -sign[d] * s, True))
+        if s == far - 1:
+            rs_sub(0, True)
         if s == 1:
             gr[...] = jnp.sum(cot[...].astype(F32), axis=0)
         for u in range(2):
@@ -251,40 +276,37 @@
                 pt(d * (far - 1) + s, u, -sign[d] * s, False).wait_recv()
         process([-s, s])
         if s == 1:
-            cxf_in.wait_recv()
-        if s >= 2:
-            scale_in(s - 2)
+            cxf.wait_recv()
+        if s < half:
+            scale_in(s - 1)
+    for n in range(1, far - 1):
+        project(theirs[n])
+    rs_sub(1, False)
     for d in range(2):
         ag(d, far, d, 1).wait_recv()
         go_send(pt(2 * far - 1, d, far, True))
     for d in range(2):
         pt(2 * far - 1, d, far, False).wait_recv()
     process([far])
-    for j in range(far - 2, half):
-        scale_in(j)
-    rs_step(0)
-
-    def project_rest(lo, hi):
-        def body(j, carry):
-            project((1 - m) * half + j)
-            return carry
-        lax.fori_loop(lo, hi, body, 0)
-
-    project_rest(0, half)
-    rs_step(1)
+    project(theirs[0])
+    for n in range(far - 1, half):
+        scale_in(n)
+        project(theirs[n])
+
+    ld_res.wait()
     resw = res[...].astype(F32)
     for e in range(E):
         pe = proj[e * T:(e + 1) * T, :]
         hid[e] = (resw + pe * outw[e:e + 1]).astype(BF16)
         arb[0, 2 * E + e:2 * E + e + 1, :] = jnp.sum(cot[e].astype(F32) * pe, axis=0, keepdims=True)
-    for j in range(half):
-        cols = slice(j * R2, (j + 1) * R2)
+    for n in range(half):
         for e in range(E):
             rows = slice(e * T, (e + 1) * T)
-            a = ctx[e, :, cols].astype(F32) * part[m * half + j, rows, :].astype(F32)
+            cols = slice(n * R2, (n + 1) * R2)
+            a = ctx[e, :, cols].astype(F32) * part[m * half + n, rows, :].astype(F32)
             arb[0, e:e + 1, cols] = jnp.sum(a, axis=0, keepdims=True)
-            a = cbuf[j, e].astype(F32) * part[(1 - m) * half + j, rows, :].astype(F32)
-            arb[0, E + e:E + e + 1, cols] = jnp.sum(a, axis=0, keepdims=True)
+            a = cbuf[n, e].astype(F32) * part[theirs[n], rows, :].astype(F32)
+            arb[0, E + e:E + e + 1, cols_of(theirs[n])] = jnp.sum(a, axis=0, keepdims=True)
 
     def ar(i):
         return rc(arb.at[i], arr.at[i], ar_ss.at[i], ar_rs.at[i], flips[i])
@@ -303,35 +325,48 @@
             gi[...] = total[:E]
             go[...] = total[2 * E:]
 
+    def finish(n):
+        chip = mine[n]
+        slot = chip % half
+        rc(xrecv.at[slot], xrecv.at[slot], px_ss.at[slot], px_rs.at[slot], peer).wait_recv()
+        for e in range(E):
+            rows = slice(e * T, (e + 1) * T)
+            be = part[chip, rows, :].astype(F32) + xrecv[slot, rows, :].astype(F32)
+            wide = inf[e:e + 1, cols_of(chip)].astype(F32)
+            gc[e, :, cols_of(chip)] = (be * wide).astype(BF16)
+
     go_send(ar(0))
+    rs_sub(1, True)
     ar_step(0)
     done = 1
+    pending = half
     for k in range(2, far):
-        rs_step(k)
-        if done < len(bits):
-            ar_step(done)
-            done += 1
+        for late in (False, True):
+            rs_sub(k, late)
+            if late and done < len(bits):
+                ar_step(done)
+                done += 1
+        if pending > 2:
+            pending -= 1
+            finish(pending)
+    ps(q).wait_recv()
+
+    def own(u):
+        rows = slice(u * S, (u + 1) * S)
+        total = chip_sum(q, u)
+        for d in range(2):
+            rs(d, far - 1, u).wait_recv()
+            total = total + rrecv[d, far - 1, rows, :].astype(F32)
+        gw[rows, :] = total
+
     while done < len(bits):
         ar_step(done)
         done += 1
-
-    ps(q).wait_recv()
-    for u in range(2):
-        rows = slice(u * S, (u + 1) * S)
-        own = chip_sum(q, u)
-        for d in range(2):
-            rs(d, far - 1, u).wait_recv()
-            own = own + rrecv[d, far - 1, rows, :].astype(F32)
-        gw[rows, :] = own
-
-    for j in range(half):
-        rc(xrecv.at[j], xrecv.at[j], px_ss.at[j], px_rs.at[j], peer).wait_recv()
-        cols = slice(j * R2, (j + 1) * R2)
-        for e in range(E):
-            rows = slice(e * T, (e + 1) * T)
-            be = part[m * half + j, rows, :].astype(F32) + xrecv[j, rows, :].astype(F32)
-            gc[e, :, cols] = (be * inw[e:e + 1, cols]).astype(BF16)
-
+    own(0)
+    own(1)
+    while pending > 0:
+        pending -= 1
+        finish(pending)
     swap.wait_recv()
     gi[...] += swp[1]
 
@@ -342,8 +377,9 @@
         ps(j).wait_send()
         return carry
     lax.fori_loop(0, C, drain, 0)
-    for j in range(half):
-        rc(part.at[(1 - m) * half + j], xrecv.at[j], px_ss.at[j], px_rs.at[j], peer).wait_send()
+    for n in range(half):
+        slot = theirs[n] % half
+        rc(part.at[theirs[n]], xrecv.at[slot], px_ss.at[slot], px_rs.at[slot], peer).wait_send()
 
 
 def fused(C, context, residual, out_weight, in_factor, out_factor, cotangent):
@@ -360,18 +396,21 @@
     results = pl.pallas_call(
         functools.partial(kernel, C),
         out_shape=(
-            shape((E, T, H), BF16),
-            shape((E, T, H), BF16),
-            shape((R, H), F32),
-            shape((E, H), F32),
-            shape((E, H), F32),
-            shape((T, H), F32),
+            pltpu.VMEM((E, T, H), BF16),
+            pltpu.VMEM((E, T, H), BF16),
+            pltpu.VMEM((R, H), F32),
+            pltpu.VMEM((E, H), F32),
+            pltpu.VMEM((E, H), F32),
+            pltpu.VMEM((T, H), F32),
         ),
-        in_specs=[hbm, vm, hbm, vm, vm, hbm],
+        in_specs=[hbm] * 6,
         out_specs=tuple([vm] * 6),
         scratch_shapes=[
             pltpu.VMEM((E, T, H), BF16),
             pltpu.VMEM((E, T, H), BF16),
+            pltpu.VMEM((T, H), BF16),
+            pltpu.VMEM((E, H), BF16),
+            pltpu.VMEM((E, H), BF16),
             pltpu.VMEM((half, E, T, 2 * R), BF16),
             pltpu.VMEM((E, H), BF16),
             pltpu.VMEM((C, M, 2 * R), BF16),
@@ -388,7 +427,7 @@
             pltpu.VMEM((steps, 3 * E, H), F32),
             pltpu.VMEM((steps, 3 * E, H), F32),
             pltpu.VMEM((2, E, H), F32),
-            dma((3,)),
+            dma((6,)),
             dma((half + 2,)),
             dma((half + 2,)),
             dma((2, far, 2)),
@@ -405,7 +444,7 @@
             dma((steps,)),
         ],
         compiler_params=pltpu.CompilerParams(
-            collective_id=0, has_side_effects=True, vmem_limit_bytes=60 * 1024 * 1024
+            collective_id=0, has_side_effects=True, vmem_limit_bytes=62208 * 1024
         ),
     )(context, residual, out_weight, in_factor, out_factor, cotangent)
     return pl.pallas_call(
@@ -413,20 +452,16 @@
         out_shape=tuple(shape(r.shape, r.dtype) for r in results),
         in_specs=[hbm] * 6,
         out_specs=tuple([hbm] * 6),
-        scratch_shapes=[pltpu.VMEM(r.shape, r.dtype) for r in results] + [dma((2, 6))],
+        scratch_shapes=[dma((6,))],
+        compiler_params=pltpu.CompilerParams(vmem_limit_bytes=1024 * 1024),
     )(*results)
 
 
 def deliver(*refs):
-    sources, results, held, sem = refs[:6], refs[6:12], refs[12:18], refs[18]
-    loads = [pltpu.make_async_copy(sources[i], held[i], sem.at[0, i]) for i in range(6)]
-    stores = [pltpu.make_async_copy(held[i], results[i], sem.at[1, i]) for i in range(6)]
-    for copy in loads:
+    copies = [pltpu.make_async_copy(refs[i], refs[6 + i], refs[12].at[i]) for i in range(6)]
+    for copy in copies:
         copy.start()
-    for i in range(6):
-        loads[i].wait()
-        stores[i].start()
-    for copy in stores:
+    for copy in copies:
         copy.wait()
 
 

time: 67.3 us -> 58.7 us (0.87)
  Pallas kernels: 66.5 us -> 57.9 us
    pallas_call x1, Pallas kernels: 63.5 us -> 56.2 us  [fused(): pl.pallas_call(functools.partial(kernel, C), out_shape=(pltpu.VMEM((E, T,...]
    pallas_call x1, Pallas kernels: 3 us -> 1.72 us  [fused(): pl.pallas_call(deliver, out_shape=tuple((shape(r.shape, r.dtype) for r in...]
where the time goes in v1:
time: 58.7 us; the launch traced here: 58.6 us
  Pallas kernels  57.9 us (99%)
  between operations  0.64 us (1%)
    pallas_call x1, Pallas kernels, fused(): pl.pallas_call(functools.partial(kernel, C), out_shape=(pltpu.VMEM((E, T,...  56.2 us
    pallas_call x1, Pallas kernels, fused(): pl.pallas_call(deliver, out_shape=tuple((shape(r.shape, r.dtype) for r in...  1.72 us

profile of v1, /device:TPU:0, one launch (start us, length us, event | category | flops | bytes accessed | tf_op | source)
XLA Modules:
  0.0 58.6 jit_solution(4480238162905170909)
XLA Ops:
  0.6 56.2 %shard_map.109 = (bf16[4,128,1024]{2,1,0:T(8,128)(2,1)S(1)}, bf16[4,128,1024]{2,1,0:T(8,128)(2,1)S(1)}, f32[128,1024]{1,0:T(8,128)S(1)}, f32[4,1024]{1,0:T(4,128...) custom-call(bf16[4,128,1024]{2,1,0:T(8,128)(2,1)} %ctx_h.1, bf16[128,1024]{1,0:T(8,128)(2,1)} %res_h.1, ...), custom_call_target="tpu_custom_call" | custom-call | tf_op jit(solution)/shard_map/pallas_call | solution.py:396
  56.8 1.7 %shard_map.110 = (bf16[4,128,1024]{2,1,0:T(8,128)(2,1)}, bf16[4,128,1024]{2,1,0:T(8,128)(2,1)}, f32[128,1024]{1,0:T(8,128)}, f32[4,1024]{1,0:T(4,128)}, f32[4,1024]{1,0:T(4,128)}, /*index=5*/f32[128,1024]{1,0:T(8,128)}) custom-call(bf16[4,128,1024]{2,1,0:T(8,128)(2,1)S(1)} %get-tuple-element.12.refs_0_, bf16[4,128,1024]{2,1,0:T(8,128)(2,1)S(1)} %get-tuple-element.13.refs_1_, ...), custom_call_target="tpu_custom_call" | custom-call | tf_op jit(solution)/shard_map/pallas_call | solution.py:450

commit v2 on v1

--- a/solution.py
+++ b/solution.py
@@ -45,9 +45,11 @@
 def kernel(
     C,
     ctx_h, res_h, w_h, inf_h, outf_h, cot_h,
+    hid_o, gc_o, gw_o, gi_o, go_o, gr_o,
     hid, gc, gw, gi, go, gr,
-    ctx, cot, res, inf, outf, cbuf, infx, sc, sg, wb, proj, part, xrecv, gall, psend, precv, rsend, rrecv, arb, arr, swp,
-    ld_sem, cx_ss, cx_rs, ag_ss, ag_rs, pt_ss, pt_rs, px_ss, px_rs, ps_ss, ps_rs, rs_ss, rs_rs, ar_ss, ar_rs,
+    ctx, cot, res, inf, outf, cbuf, infx, sc, sg, wb, proj, part, xrecv, gall, psend, precv, rsend, rrecv,
+    arb, ars, arr, fin, swp, swr,
+    ld_sem, st_sem, out_sem, cx_rs, ag_rs, pt_rs, px_rs, ps_rs, rs_rs, ar_rs,
 ):
     E, T, H = ctx.shape
     R = w_h.shape[0]
@@ -55,11 +57,9 @@
     S = R // 2
     half = C // 2
     far = C // 2
-    bits = []
-    b = 1
-    while b < 2 * C:
-        bits.append(b)
-        b *= 2
+    lines = C // 2
+    H2 = H // 2
+    pieces = 2 * far - 1
 
     m = lax.axis_index("member")
     f = lax.axis_index("fsdp")
@@ -78,7 +78,19 @@
     prv = (m, chip_at(-1) * 2 + c)
     side = (nxt, prv)
     sign = (1, -1)
-    flips = [(m, f + bit * (1 - 2 * ((f // bit) % 2))) for bit in bits]
+    cross = (1 - m, q * 2 + 1 - c)
+    beside = (m, f + 2 - 4 * (q % 2))
+
+    def along(i):
+        line = q // 2
+        other = 0
+        bit = 1
+        while bit < lines:
+            own = (line // bit) % 2
+            other = other + bit * (1 - own if i & bit else own)
+            bit *= 2
+        return (m, f + 4 * (other - line))
+
 
     def rc(src, dst, ss, rs, dev):
         return pltpu.make_async_remote_copy(
@@ -98,6 +110,11 @@
         copy = pltpu.make_async_copy(src, dst, ld_sem.at[i])
         copy.start()
         return copy
+
+    def store(i, src, dst):
+        pltpu.make_async_copy(src, dst, st_sem.at[i]).start()
+
+    CX, CXF, AG, PT, PX, PS, RS, AR, SWAP, FIN = range(10)
 
     ld_inf = load(0, inf_h, inf)
     ld_ctx = load(1, ctx_h, ctx)
@@ -125,42 +142,41 @@
         return pl.ds(pl.multiple_of((chip % half) * R2, R2), R2)
 
     def cx(n):
-        return rc(ctx_h.at[:, :, cols_of(mine[n])], cbuf.at[n], cx_ss.at[n], cx_rs.at[n], peer)
-
-    cxf = rc(inf_h, infx, cx_ss.at[half], cx_rs.at[half], peer)
+        return rc(ctx_h.at[:, :, cols_of(mine[n])], cbuf.at[n], out_sem.at[CX], cx_rs.at[n], peer)
+
+    cxf = rc(inf_h, infx, out_sem.at[CXF], cx_rs.at[half], peer)
 
     def sub(core, u):
         return pl.ds(pl.multiple_of(core * R + u * S, S), S)
-
-    def subs(d, s):
-        return (0, 1) if s < far else (d,)
 
     def ag(d, s, u, shift):
         qq = chip_at(-sign[d] * (s - 1 + shift))
         dst = wb.at[qq, sub(c, u)]
         src = w_h.at[pl.ds(u * S, S)] if (s == 1 and shift == 0) else dst
-        return rc(src, dst, ag_ss.at[d, s - 1, u], ag_rs.at[d, s - 1, u], side[d])
-
-    def pt(k, u, offset, own):
+        return rc(src, dst, out_sem.at[AG], ag_rs.at[2 * (s - 1) + int(u != d)], side[d])
+
+    def pt(s, u, offset, own):
         qq = chip_at(offset)
         dst = wb.at[qq, sub(c if own else 1 - c, u)]
-        src = w_h.at[pl.ds(u * S, S)] if (own and k == 0) else dst
-        return rc(src, dst, pt_ss.at[k, u], pt_rs.at[k, u], partner)
-
-    sends = []
-
-    def go_send(copy):
-        copy.start()
-        sends.append(copy)
+        src = w_h.at[pl.ds(u * S, S)] if (own and s == 0) else dst
+        return rc(src, dst, out_sem.at[PT], pt_rs.at[s], partner)
+
+    def both_wait(sems, i):
+        held = wb.at[q, rows_of(c)]
+        rc(held, held, out_sem.at[AG], sems.at[i], nxt).wait_recv()
+
+    def pt_wait(s):
+        held = wb.at[q] if 0 < s < far else wb.at[q, rows_of(c)]
+        rc(held, held, out_sem.at[PT], pt_rs.at[s], partner).wait_recv()
 
     pl.semaphore_wait(barrier, len(greet))
-    go_send(cxf)
+    cxf.start()
     for n in range(half):
-        go_send(cx(n))
-    for u in range(2):
+        cx(n).start()
+    for t in range(2):
         for d in range(2):
-            go_send(ag(d, 1, u, 0))
-        go_send(pt(0, u, 0, True))
+            ag(d, 1, d if t == 0 else 1 - d, 0).start()
+        pt(0, t, 0, True).start()
 
     ld_inf.wait()
     ld_ctx.wait()
@@ -176,10 +192,10 @@
         sg[e * T:(e + 1) * T, :] = (cot[e].astype(F32) * outw[e:e + 1]).astype(BF16)
 
     def px(qq):
-        return rc(part.at[qq], xrecv.at[qq % half], px_ss.at[qq % half], px_rs.at[qq % half], peer)
+        return rc(part.at[qq], xrecv.at[qq % half], out_sem.at[PX], px_rs.at[qq % half], peer)
 
     def ps(qq):
-        return rc(psend.at[qq], precv.at[qq], ps_ss.at[qq], ps_rs.at[qq], partner)
+        return rc(psend.at[qq], precv.at[qq], out_sem.at[PS], ps_rs.at[qq], partner)
 
     def gw_one(qq):
         g = lax.dot_general(sc[qq], sg[...], (((0,), (0,)), ((), ())), preferred_element_type=F32)
@@ -222,35 +238,39 @@
             return carry
         lax.fori_loop(0, len(offsets), body, 0)
 
+    def piece(k, u, d):
+        return 2 * k - 1 + int(u == d) if k else 0
+
     def rs(d, k, u):
-        rows = pl.ds(u * S, S)
-        return rc(rsend.at[d, k, rows], rrecv.at[d, k, rows], rs_ss.at[d, k, u], rs_rs.at[d, k, u], side[d])
+        i = piece(k, u, d)
+        return rc(rsend.at[d, i], rrecv.at[d, i], out_sem.at[RS], rs_rs.at[i], side[d])
 
     def chip_sum(qq, u):
         rows = slice(u * S, (u + 1) * S)
         return gall[qq, c, rows, :] + precv[qq, rows, :].astype(F32)
 
     def rs_sub(k, late):
+        chips = [chip_at(sign[d] * (far - k)) if k else chip_at(-far) for d in range(2)]
         if k == 0:
-            ps(chip_at(-far)).wait_recv()
+            ps(chips[0]).wait_recv()
+        elif not late:
+            for d in range(2):
+                ps(chips[d]).wait_recv()
+        held = k > 1 or (k == 1 and late)
+        if held:
+            both_wait(rs_rs, piece(k - 1, int(late), 1))
         for d in range(2):
-            qq = chip_at(sign[d] * (far - k)) if k else chip_at(-far)
-            if k and not late:
-                ps(qq).wait_recv()
             u = d if late else 1 - d
-            rows = slice(u * S, (u + 1) * S)
-            v = chip_sum(qq, u)
-            if k > 1 or (k == 1 and late):
-                rs(d, k - 1, u).wait_recv()
-                v = v + rrecv[d, k - 1, rows, :].astype(F32)
-            rsend[d, k, rows, :] = v.astype(BF16)
-            go_send(rs(d, k, u))
+            v = chip_sum(chips[d], u)
+            if held:
+                v = v + rrecv[d, piece(k - 1, u, d)].astype(F32)
+            rsend[d, piece(k, u, d)] = v.astype(BF16)
+            rs(d, k, u).start()
 
     proj[...] = jnp.zeros(proj.shape, F32)
     gw_mine()
     ld_w.wait()
-    for u in range(2):
-        pt(0, u, 0, False).wait_recv()
+    pt_wait(0)
     process([0])
 
     def scale_in(n):
@@ -260,35 +280,43 @@
             sc[theirs[n], e * T:(e + 1) * T, :] = (cbuf[n, e].astype(F32) * wide).astype(BF16)
         gw_one(theirs[n])
 
+    def forward(s, t):
+        both_wait(ag_rs, 2 * (s - 1) + t)
+        for d in range(2):
+            u = d if t == 0 else 1 - d
+            if s + 1 < far or (s + 1 == far and t == 0):
+                ag(d, s + 1, u, 0).start()
+            pt(s, u, -sign[d] * s, True).start()
+
     for s in range(1, far):
-        for u in range(2):
-            for d in range(2):
-                ag(d, s, u, 1).wait_recv()
-                if u in subs(d, s + 1):
-                    go_send(ag(d, s + 1, u, 0))
-                go_send(pt(d * (far - 1) + s, u, -sign[d] * s, True))
+        forward(s, 0)
         if s == far - 1:
             rs_sub(0, True)
         if s == 1:
             gr[...] = jnp.sum(cot[...].astype(F32), axis=0)
-        for u in range(2):
-            for d in range(2):
-                pt(d * (far - 1) + s, u, -sign[d] * s, False).wait_recv()
-        process([-s, s])
-        if s == 1:
-            cxf.wait_recv()
-        if s < half:
-            scale_in(s - 1)
-    for n in range(1, far - 1):
+            store(1, gr, gr_o)
+        else:
+            pt_wait(s - 1)
+            process([1 - s])
+        forward(s, 1)
+        if s > 1:
+            process([s - 1])
+            if s == 2:
+                cxf.wait_recv()
+            scale_in(s - 2)
+    scale_in(far - 2)
+    both_wait(ag_rs, 2 * (far - 1))
+    for d in range(2):
+        pt(far, d, far, True).start()
+    pt_wait(far - 1)
+    process([1 - far])
+    rs_sub(1, False)
+    process([far - 1])
+    pt_wait(far)
+    process([far])
+    for n in range(far - 1):
         project(theirs[n])
-    rs_sub(1, False)
-    for d in range(2):
-        ag(d, far, d, 1).wait_recv()
-        go_send(pt(2 * far - 1, d, far, True))
-    for d in range(2):
-        pt(2 * far - 1, d, far, False).wait_recv()
-    process([far])
-    project(theirs[0])
+    rs_sub(1, True)
     for n in range(far - 1, half):
         scale_in(n)
         project(theirs[n])
@@ -298,88 +326,114 @@
     for e in range(E):
         pe = proj[e * T:(e + 1) * T, :]
         hid[e] = (resw + pe * outw[e:e + 1]).astype(BF16)
-        arb[0, 2 * E + e:2 * E + e + 1, :] = jnp.sum(cot[e].astype(F32) * pe, axis=0, keepdims=True)
+        a = jnp.sum(cot[e].astype(F32) * pe, axis=0, keepdims=True)
+        for h in range(2):
+            arb[h, 2 * E + e:2 * E + e + 1, :] = a[:, h * H2:(h + 1) * H2]
+    store(0, hid, hid_o)
     for n in range(half):
+        h, first = n * R2 // H2, n * R2 % H2
+        slot = theirs[n] % half
+        ahead = slot * R2 // H2
+        far_cols = pl.ds(pl.multiple_of(slot * R2 - ahead * H2, R2), R2)
         for e in range(E):
             rows = slice(e * T, (e + 1) * T)
-            cols = slice(n * R2, (n + 1) * R2)
-            a = ctx[e, :, cols].astype(F32) * part[m * half + n, rows, :].astype(F32)
-            arb[0, e:e + 1, cols] = jnp.sum(a, axis=0, keepdims=True)
+            a = ctx[e, :, n * R2:(n + 1) * R2].astype(F32) * part[m * half + n, rows, :].astype(F32)
+            arb[h, e:e + 1, first:first + R2] = jnp.sum(a, axis=0, keepdims=True)
             a = cbuf[n, e].astype(F32) * part[theirs[n], rows, :].astype(F32)
-            arb[0, E + e:E + e + 1, cols_of(theirs[n])] = jnp.sum(a, axis=0, keepdims=True)
-
-    def ar(i):
-        return rc(arb.at[i], arr.at[i], ar_ss.at[i], ar_rs.at[i], flips[i])
-
-    swap = rc(swp.at[0], swp.at[1], cx_ss.at[half + 1], cx_rs.at[half + 1], peer)
+            arb[ahead, E + e:E + e + 1, far_cols] = jnp.sum(a, axis=0, keepdims=True)
+
+    def ar(i, src, dev):
+        return rc(src, arr.at[i], out_sem.at[AR], ar_rs.at[min(i, 2)], dev)
+
+    to_partner = ar(0, arb.at[1 - c], partner)
+    to_beside = ar(1, ars.at[0], beside)
+    to_lines = [ar(1 + i, ars.at[1], along(i)) for i in range(1, lines)]
+    from_lines = rc(arr.at[2:], arr.at[2:], out_sem.at[AR], ar_rs.at[2], partner)
+    all_sums = rc(arr, arr, out_sem.at[AR], ar_rs.at[2], partner)
+    to_other = rc(fin.at[0], fin.at[1], out_sem.at[FIN], ar_rs.at[3], partner)
+    swaps = [rc(swp, swr.at[c], out_sem.at[SWAP], ar_rs.at[4], dev) for dev in (peer, cross)]
+    both_swaps = rc(swr, swr, out_sem.at[SWAP], ar_rs.at[4], peer)
+
+    own_half = pl.ds(pl.multiple_of(c * H2, H2), H2)
+    other_half = pl.ds(pl.multiple_of((1 - c) * H2, H2), H2)
 
     def ar_step(i):
-        ar(i).wait_recv()
-        total = arb[i] + arr[i]
-        if i + 1 < len(bits):
-            arb[i + 1] = total
-            go_send(ar(i + 1))
+        if i == 0:
+            to_partner.wait_recv()
+            ars[0] = arb[c] + arr[0]
+            to_beside.start()
+        elif i == 1:
+            to_beside.wait_recv()
+            ars[1] = ars[0] + arr[1]
+            for copy in to_lines:
+                copy.start()
         else:
-            swp[0] = total[E:2 * E]
-            go_send(swap)
-            gi[...] = total[:E]
-            go[...] = total[2 * E:]
+            from_lines.wait_recv()
+            total = ars[1]
+            for n in range(2, lines + 1):
+                total = total + arr[n]
+            swp[...] = total[E:2 * E]
+            fin[0, :E] = total[:E]
+            fin[0, E:] = total[2 * E:]
+            for copy in swaps:
+                copy.start()
+            to_other.start()
 
     def finish(n):
         chip = mine[n]
         slot = chip % half
-        rc(xrecv.at[slot], xrecv.at[slot], px_ss.at[slot], px_rs.at[slot], peer).wait_recv()
+        rc(xrecv.at[slot], xrecv.at[slot], out_sem.at[PX], px_rs.at[slot], peer).wait_recv()
         for e in range(E):
             rows = slice(e * T, (e + 1) * T)
             be = part[chip, rows, :].astype(F32) + xrecv[slot, rows, :].astype(F32)
             wide = inf[e:e + 1, cols_of(chip)].astype(F32)
             gc[e, :, cols_of(chip)] = (be * wide).astype(BF16)
-
-    go_send(ar(0))
-    rs_sub(1, True)
-    ar_step(0)
-    done = 1
+        store(2, gc.at[:, :, cols_of(chip)], gc_o.at[:, :, cols_of(chip)])
+
+    to_partner.start()
     pending = half
     for k in range(2, far):
-        for late in (False, True):
-            rs_sub(k, late)
-            if late and done < len(bits):
-                ar_step(done)
-                done += 1
+        rs_sub(k, False)
+        if k == 2:
+            ar_step(0)
+        rs_sub(k, True)
+        if k == 2:
+            ar_step(1)
         if pending > 2:
             pending -= 1
             finish(pending)
+    ar_step(2)
     ps(q).wait_recv()
-
-    def own(u):
+    for t in range(2):
+        both_wait(rs_rs, piece(far - 1, t, 1))
+    for u in range(2):
         rows = slice(u * S, (u + 1) * S)
         total = chip_sum(q, u)
         for d in range(2):
-            rs(d, far - 1, u).wait_recv()
-            total = total + rrecv[d, far - 1, rows, :].astype(F32)
+            total = total + rrecv[d, piece(far - 1, u, d)].astype(F32)
         gw[rows, :] = total
-
-    while done < len(bits):
-        ar_step(done)
-        done += 1
-    own(0)
-    own(1)
+        store(3, gw.at[pl.ds(u * S, S)], gw_o.at[pl.ds(u * S, S)])
+    to_other.wait_recv()
+    go[:, own_half] = fin[0, E:]
+    go[:, other_half] = fin[1, E:]
+    store(4, go, go_o)
     while pending > 0:
         pending -= 1
         finish(pending)
-    swap.wait_recv()
-    gi[...] += swp[1]
-
-    for copy in sends:
-        copy.wait_send()
-
-    def drain(j, carry):
-        ps(j).wait_send()
-        return carry
-    lax.fori_loop(0, C, drain, 0)
-    for n in range(half):
-        slot = theirs[n] % half
-        rc(part.at[theirs[n]], xrecv.at[slot], px_ss.at[slot], px_rs.at[slot], peer).wait_send()
+    both_swaps.wait_recv()
+    gi[:, own_half] = fin[0, :E] + swr[c]
+    gi[:, other_half] = fin[1, :E] + swr[1 - c]
+    store(5, gi, gi_o)
+
+    sent = (
+        (CX, cbuf), (CXF, infx), (AG, rsend), (PT, psend), (PX, xrecv),
+        (PS, psend), (RS, rsend), (AR, arr), (SWAP, swr), (FIN, fin.at[0]),
+    )
+    for i, ref in sent:
+        rc(ref, ref, out_sem.at[i], ar_rs.at[4], peer).wait_send()
+    stored = ((hid, hid_o), (gr, gr_o), (gc, gc_o), (gw, gw_o), (go, go_o), (gi, gi_o))
+    for i, (src, dst) in enumerate(stored):
+        pltpu.make_async_copy(src, dst, st_sem.at[i]).wait()
 
 
 def fused(C, context, residual, out_weight, in_factor, out_factor, cotangent):
@@ -388,8 +442,8 @@
     R = out_weight.shape[0]
     half = C // 2
     far = half
-    steps = (2 * C).bit_length() - 1
-    vm = pl.BlockSpec(memory_space=pltpu.VMEM)
+    lines = C // 2
+    pieces = 2 * far - 1
     hbm = pl.BlockSpec(memory_space=pl.ANY)
     dma = pltpu.SemaphoreType.DMA
     shape = jax.ShapeDtypeStruct
@@ -404,8 +458,14 @@
             pltpu.VMEM((T, H), F32),
         ),
         in_specs=[hbm] * 6,
-        out_specs=tuple([vm] * 6),
+        out_specs=tuple([hbm] * 6),
         scratch_shapes=[
+            pltpu.VMEM((E, T, H), BF16),
+            pltpu.VMEM((E, T, H), BF16),
+            pltpu.VMEM((R, H), F32),
+            pltpu.VMEM((E, H), F32),
+            pltpu.VMEM((E, H), F32),
+            pltpu.VMEM((T, H), F32),
             pltpu.VMEM((E, T, H), BF16),
             pltpu.VMEM((E, T, H), BF16),
             pltpu.VMEM((T, H), BF16),
@@ -422,26 +482,24 @@
             pltpu.VMEM((C, 2, R, H), F32),
             pltpu.VMEM((C, R, H), BF16),
             pltpu.VMEM((C, R, H), BF16),
-            pltpu.VMEM((2, far, R, H), BF16),
-            pltpu.VMEM((2, far, R, H), BF16),
-            pltpu.VMEM((steps, 3 * E, H), F32),
-            pltpu.VMEM((steps, 3 * E, H), F32),
-            pltpu.VMEM((2, E, H), F32),
+            pltpu.VMEM((2, pieces, R // 2, H), BF16),
+            pltpu.VMEM((2, pieces, R // 2, H), BF16),
+            pltpu.VMEM((2, 3 * E, H // 2), F32),
+            pltpu.VMEM((2, 3 * E, H // 2), F32),
+            pltpu.VMEM((lines + 1, 3 * E, H // 2), F32),
+            pltpu.VMEM((2, 2 * E, H // 2), F32),
+            pltpu.VMEM((E, H // 2), F32),
+            pltpu.VMEM((2, E, H // 2), F32),
             dma((6,)),
-            dma((half + 2,)),
-            dma((half + 2,)),
-            dma((2, far, 2)),
-            dma((2, far, 2)),
-            dma((2 * far, 2)),
-            dma((2 * far, 2)),
-            dma((half,)),
+            dma((6,)),
+            dma((10,)),
+            dma((half + 1,)),
+            dma((pieces,)),
+            dma((far + 1,)),
             dma((half,)),
             dma((C,)),
-            dma((C,)),
-            dma((2, far, 2)),
-            dma((2, far, 2)),
-            dma((steps,)),
-            dma((steps,)),
+            dma((pieces,)),
+            dma((5,)),
         ],
         compiler_params=pltpu.CompilerParams(
             collective_id=0, has_side_effects=True, vmem_limit_bytes=62208 * 1024

time: 58.7 us -> 53.8 us (0.917)
  Pallas kernels: 57.9 us -> 53 us
    pallas_call x1, Pallas kernels: 56.2 us -> 51.3 us  [fused(): pl.pallas_call(functools.partial(kernel, C), out_shape=(pltpu.VMEM((E, T,...]
where the time goes in v2:
time: 53.8 us; the launch traced here: 53.6 us
  Pallas kernels  53 us (99%)
  between operations  0.64 us (1%)
    pallas_call x1, Pallas kernels, fused(): pl.pallas_call(functools.partial(kernel, C), out_shape=(pltpu.VMEM((E, T,...  51.3 us
    pallas_call x1, Pallas kernels, fused(): pl.pallas_call(deliver, out_shape=tuple((shape(r.shape, r.dtype) for r in...  1.72 us

profile of v2, /device:TPU:0, one launch (start us, length us, event | category | flops | bytes accessed | tf_op | source)
XLA Modules:
  0.0 53.6 jit_solution(17420194072938363043)
XLA Ops:
  0.6 51.3 %shard_map.109 = (bf16[4,128,1024]{2,1,0:T(8,128)(2,1)S(1)}, bf16[4,128,1024]{2,1,0:T(8,128)(2,1)S(1)}, f32[128,1024]{1,0:T(8,128)S(1)}, f32[4,1024]{1,0:T(4,128...) custom-call(bf16[4,128,1024]{2,1,0:T(8,128)(2,1)} %ctx_h.1, bf16[128,1024]{1,0:T(8,128)(2,1)} %res_h.1, ...), custom_call_target="tpu_custom_call" | custom-call | tf_op jit(solution)/shard_map/pallas_call | solution.py:450
  51.9 1.7 %shard_map.110 = (bf16[4,128,1024]{2,1,0:T(8,128)(2,1)}, bf16[4,128,1024]{2,1,0:T(8,128)(2,1)}, f32[128,1024]{1,0:T(8,128)}, f32[4,1024]{1,0:T(4,128)}, f32[4,1024]{1,0:T(4,128)}, /*index=5*/f32[128,1024]{1,0:T(8,128)}) custom-call(bf16[4,128,1024]{2,1,0:T(8,128)(2,1)S(1)} %get-tuple-element.12.refs_0_, bf16[4,128,1024]{2,1,0:T(8,128)(2,1)S(1)} %get-tuple-element.13.refs_1_, ...), custom_call_target="tpu_custom_call" | custom-call | tf_op jit(solution)/shard_map/pallas_call | solution.py:508

commit v3 on v2

--- a/solution.py
+++ b/solution.py
@@ -49,7 +49,32 @@
     hid, gc, gw, gi, go, gr,
     ctx, cot, res, inf, outf, cbuf, infx, sc, sg, wb, proj, part, xrecv, gall, psend, precv, rsend, rrecv,
     arb, ars, arr, fin, swp, swr,
-    ld_sem, st_sem, out_sem, cx_rs, ag_rs, pt_rs, px_rs, ps_rs, rs_rs, ar_rs,
+    cx_rs, ag_rs, pt_rs, px_rs, ps_rs, rs_rs, ar_rs, ready,
+):
+    dma = pltpu.SemaphoreType.DMA
+    pl.run_scoped(
+        functools.partial(
+            work, C,
+            ctx_h, res_h, w_h, inf_h, outf_h, cot_h,
+            hid_o, gc_o, gw_o, gi_o, go_o, gr_o,
+            hid, gc, gw, gi, go, gr,
+            ctx, cot, res, inf, outf, cbuf, infx, sc, sg, wb, proj, part, xrecv, gall, psend, precv, rsend, rrecv,
+            arb, ars, arr, fin, swp, swr,
+            cx_rs, ag_rs, pt_rs, px_rs, ps_rs, rs_rs, ar_rs, ready,
+        ),
+        dma((6,)), dma((6,)), dma((10,)),
+    )
+
+
+def work(
+    C,
+    ctx_h, res_h, w_h, inf_h, outf_h, cot_h,
+    hid_o, gc_o, gw_o, gi_o, go_o, gr_o,
+    hid, gc, gw, gi, go, gr,
+    ctx, cot, res, inf, outf, cbuf, infx, sc, sg, wb, proj, part, xrecv, gall, psend, precv, rsend, rrecv,
+    arb, ars, arr, fin, swp, swr,
+    cx_rs, ag_rs, pt_rs, px_rs, ps_rs, rs_rs, ar_rs, ready,
+    ld_sem, st_sem, out_sem,
 ):
     E, T, H = ctx.shape
     R = w_h.shape[0]
@@ -99,9 +124,19 @@
         )
 
     barrier = pltpu.get_barrier_semaphore()
-    greet = [peer, partner, nxt, prv]
-    for dev in greet:
+
+    def greet(dev):
         pl.semaphore_signal(barrier, inc=1, device_id=dev, device_id_type=pl.DeviceIdType.MESH)
+
+    lead, deputy = m * (1 - c) == 1, m * c == 1
+    greet((1 - m, q * 2 + m * c))
+
+    @pl.when(jnp.logical_not(lead))
+    def _():
+        greet(partner)
+
+    for ahead in (1, -1):
+        greet((m, chip_at(ahead) * 2 + c + m * (1 - c)))
 
     def rows_of(core):
         return pl.ds(pl.multiple_of(core * R, R), R)
@@ -169,10 +204,34 @@
         held = wb.at[q] if 0 < s < far else wb.at[q, rows_of(c)]
         rc(held, held, out_sem.at[PT], pt_rs.at[s], partner).wait_recv()
 
-    pl.semaphore_wait(barrier, len(greet))
+    def tell(sem):
+        pl.semaphore_signal(sem, inc=1, device_id=partner, device_id_type=pl.DeviceIdType.MESH)
+
+    @pl.when(jnp.logical_not(deputy))
+    def _():
+        pl.semaphore_wait(barrier, 4 - m)
+
+    @pl.when(lead)
+    def _():
+        tell(ready)
+
+    @pl.when(deputy)
+    def _():
+        pl.semaphore_wait(ready, 1)
+
     cxf.start()
     for n in range(half):
         cx(n).start()
+
+    @pl.when(deputy)
+    def _():
+        pl.semaphore_wait(barrier, 4)
+        tell(ready)
+
+    @pl.when(lead)
+    def _():
+        pl.semaphore_wait(ready, 1)
+
     for t in range(2):
         for d in range(2):
             ag(d, 1, d if t == 0 else 1 - d, 0).start()
@@ -191,8 +250,9 @@
     for e in range(E):
         sg[e * T:(e + 1) * T, :] = (cot[e].astype(F32) * outw[e:e + 1]).astype(BF16)
 
-    def px(qq):
-        return rc(part.at[qq], xrecv.at[qq % half], out_sem.at[PX], px_rs.at[qq % half], peer)
+    def px(qq, first):
+        rows = pl.ds(0 if first else E * T // 2, E * T // 2)
+        return rc(part.at[qq, rows], xrecv.at[qq % half, rows], out_sem.at[PX], px_rs.at[qq % half], peer)
 
     def ps(qq):
         return rc(psend.at[qq], precv.at[qq], out_sem.at[PS], ps_rs.at[qq], partner)
@@ -230,7 +290,11 @@
 
             @pl.when(qq // half != m)
             def _():
-                px(qq).start()
+                px(qq, True).start()
+
+            @pl.when(jnp.logical_and(qq // half != m, qq != theirs[0]))
+            def _():
+                px(qq, False).start()
 
             @pl.when(qq // half == m)
             def _():
@@ -349,7 +413,6 @@
     to_beside = ar(1, ars.at[0], beside)
     to_lines = [ar(1 + i, ars.at[1], along(i)) for i in range(1, lines)]
     from_lines = rc(arr.at[2:], arr.at[2:], out_sem.at[AR], ar_rs.at[2], partner)
-    all_sums = rc(arr, arr, out_sem.at[AR], ar_rs.at[2], partner)
     to_other = rc(fin.at[0], fin.at[1], out_sem.at[FIN], ar_rs.at[3], partner)
     swaps = [rc(swp, swr.at[c], out_sem.at[SWAP], ar_rs.at[4], dev) for dev in (peer, cross)]
     both_swaps = rc(swr, swr, out_sem.at[SWAP], ar_rs.at[4], peer)
@@ -403,6 +466,7 @@
             pending -= 1
             finish(pending)
     ar_step(2)
+    px(theirs[0], False).start()
     ps(q).wait_recv()
     for t in range(2):
         both_wait(rs_rs, piece(far - 1, t, 1))
@@ -490,9 +554,6 @@
             pltpu.VMEM((2, 2 * E, H // 2), F32),
             pltpu.VMEM((E, H // 2), F32),
             pltpu.VMEM((2, E, H // 2), F32),
-            dma((6,)),
-            dma((6,)),
-            dma((10,)),
             dma((half + 1,)),
             dma((pieces,)),
             dma((far + 1,)),
@@ -500,6 +561,7 @@
             dma((C,)),
             dma((pieces,)),
             dma((5,)),
+            pltpu.SemaphoreType.REGULAR,
         ],
         compiler_params=pltpu.CompilerParams(
             collective_id=0, has_side_effects=True, vmem_limit_bytes=62208 * 1024

time: 53.8 us -> 53.3 us (level)
  no operation moved by 1% of the time
where the time goes in v3:
time: 53.3 us; the launch traced here: 53.2 us
  Pallas kernels  52.5 us (98%)
  between operations  0.64 us (1%)
    pallas_call x1, Pallas kernels, fused(): pl.pallas_call(functools.partial(kernel, C), out_shape=(pltpu.VMEM((E, T,...  50.8 us
    pallas_call x1, Pallas kernels, fused(): pl.pallas_call(deliver, out_shape=tuple((shape(r.shape, r.dtype) for r in...  1.72 us

profile of v3, /device:TPU:0, one launch (start us, length us, event | category | flops | bytes accessed | tf_op | source)
XLA Modules:
  0.0 53.2 jit_solution(13833383140555555372)
XLA Ops:
  0.6 50.8 %shard_map.109 = (bf16[4,128,1024]{2,1,0:T(8,128)(2,1)S(1)}, bf16[4,128,1024]{2,1,0:T(8,128)(2,1)S(1)}, f32[128,1024]{1,0:T(8,128)S(1)}, f32[4,1024]{1,0:T(4,128...) custom-call(bf16[4,128,1024]{2,1,0:T(8,128)(2,1)} %ctx_h.1, bf16[128,1024]{1,0:T(8,128)(2,1)} %res_h.1, ...), custom_call_target="tpu_custom_call" | custom-call | tf_op jit(solution)/shard_map/pallas_call | solution.py:514
  51.5 1.7 %shard_map.110 = (bf16[4,128,1024]{2,1,0:T(8,128)(2,1)}, bf16[4,128,1024]{2,1,0:T(8,128)(2,1)}, f32[128,1024]{1,0:T(8,128)}, f32[4,1024]{1,0:T(4,128)}, f32[4,1024]{1,0:T(4,128)}, /*index=5*/f32[128,1024]{1,0:T(8,128)}) custom-call(bf16[4,128,1024]{2,1,0:T(8,128)(2,1)S(1)} %get-tuple-element.12.refs_0_, bf16[4,128,1024]{2,1,0:T(8,128)(2,1)S(1)} %get-tuple-element.13.refs_1_, ...), custom_call_target="tpu_custom_call" | custom-call | tf_op jit(solution)/shard_map/pallas_call | solution.py:570

commit v4 on v3

--- a/solution.py
+++ b/solution.py
@@ -42,27 +42,23 @@
     return (hidden, grad_context, grad_weight, grad_in, grad_out, grad_residual)
 
 
-def kernel(
-    C,
-    ctx_h, res_h, w_h, inf_h, outf_h, cot_h,
-    hid_o, gc_o, gw_o, gi_o, go_o, gr_o,
-    hid, gc, gw, gi, go, gr,
-    ctx, cot, res, inf, outf, cbuf, infx, sc, sg, wb, proj, part, xrecv, gall, psend, precv, rsend, rrecv,
-    arb, ars, arr, fin, swp, swr,
-    cx_rs, ag_rs, pt_rs, px_rs, ps_rs, rs_rs, ar_rs, ready,
-):
+def kernel(C, *refs):
+    half = C // 2
+    far = C // 2
     dma = pltpu.SemaphoreType.DMA
     pl.run_scoped(
-        functools.partial(
-            work, C,
-            ctx_h, res_h, w_h, inf_h, outf_h, cot_h,
-            hid_o, gc_o, gw_o, gi_o, go_o, gr_o,
-            hid, gc, gw, gi, go, gr,
-            ctx, cot, res, inf, outf, cbuf, infx, sc, sg, wb, proj, part, xrecv, gall, psend, precv, rsend, rrecv,
-            arb, ars, arr, fin, swp, swr,
-            cx_rs, ag_rs, pt_rs, px_rs, ps_rs, rs_rs, ar_rs, ready,
-        ),
-        dma((6,)), dma((6,)), dma((10,)),
+        functools.partial(work, C, *refs),
+        dma((6,)),
+        dma((6,)),
+        dma((10,)),
+        dma((half + 1,)),
+        dma((2 * far - 1,)),
+        dma((far + 1,)),
+        dma((half + 1,)),
+        dma((C,)),
+        dma((2 * far - 1,)),
+        dma((5,)),
+        pltpu.SemaphoreType.REGULAR,
     )
 
 
@@ -73,8 +69,7 @@
     hid, gc, gw, gi, go, gr,
     ctx, cot, res, inf, outf, cbuf, infx, sc, sg, wb, proj, part, xrecv, gall, psend, precv, rsend, rrecv,
     arb, ars, arr, fin, swp, swr,
-    cx_rs, ag_rs, pt_rs, px_rs, ps_rs, rs_rs, ar_rs, ready,
-    ld_sem, st_sem, out_sem,
+    ld_sem, st_sem, out_sem, cx_rs, ag_rs, pt_rs, px_rs, ps_rs, rs_rs, ar_rs, ready,
 ):
     E, T, H = ctx.shape
     R = w_h.shape[0]
@@ -250,9 +245,10 @@
     for e in range(E):
         sg[e * T:(e + 1) * T, :] = (cot[e].astype(F32) * outw[e:e + 1]).astype(BF16)
 
-    def px(qq, first):
+    def px(qq, first, last=False):
         rows = pl.ds(0 if first else E * T // 2, E * T // 2)
-        return rc(part.at[qq, rows], xrecv.at[qq % half, rows], out_sem.at[PX], px_rs.at[qq % half], peer)
+        i = half if last else qq % half
+        return rc(part.at[qq, rows], xrecv.at[qq % half, rows], out_sem.at[PX], px_rs.at[i], peer)
 
     def ps(qq):
         return rc(psend.at[qq], precv.at[qq], out_sem.at[PS], ps_rs.at[qq], partner)
@@ -442,16 +438,20 @@
                 copy.start()
             to_other.start()
 
-    def finish(n):
+    def finish(n, members, i):
         chip = mine[n]
         slot = chip % half
-        rc(xrecv.at[slot], xrecv.at[slot], out_sem.at[PX], px_rs.at[slot], peer).wait_recv()
-        for e in range(E):
+        held = xrecv.at[slot, pl.ds(members[0] * T, len(members) * T)]
+        rc(held, held, out_sem.at[PX], px_rs.at[i], peer).wait_recv()
+        for e in members:
             rows = slice(e * T, (e + 1) * T)
             be = part[chip, rows, :].astype(F32) + xrecv[slot, rows, :].astype(F32)
             wide = inf[e:e + 1, cols_of(chip)].astype(F32)
             gc[e, :, cols_of(chip)] = (be * wide).astype(BF16)
-        store(2, gc.at[:, :, cols_of(chip)], gc_o.at[:, :, cols_of(chip)])
+        rows = pl.ds(members[0], len(members))
+        store(2, gc.at[rows, :, cols_of(chip)], gc_o.at[rows, :, cols_of(chip)])
+
+    every = range(E)
 
     to_partner.start()
     pending = half
@@ -464,9 +464,9 @@
             ar_step(1)
         if pending > 2:
             pending -= 1
-            finish(pending)
+            finish(pending, every, mine[pending] % half)
     ar_step(2)
-    px(theirs[0], False).start()
+    px(theirs[0], False, True).start()
     ps(q).wait_recv()
     for t in range(2):
         both_wait(rs_rs, piece(far - 1, t, 1))
@@ -481,9 +481,11 @@
     go[:, own_half] = fin[0, E:]
     go[:, other_half] = fin[1, E:]
     store(4, go, go_o)
-    while pending > 0:
+    while pending > 1:
         pending -= 1
-        finish(pending)
+        finish(pending, every, mine[pending] % half)
+    finish(0, every[:E // 2], mine[0] % half)
+    finish(0, every[E // 2:], half)
     both_swaps.wait_recv()
     gi[:, own_half] = fin[0, :E] + swr[c]
     gi[:, other_half] = fin[1, :E] + swr[1 - c]
@@ -509,7 +511,6 @@
     lines = C // 2
     pieces = 2 * far - 1
     hbm = pl.BlockSpec(memory_space=pl.ANY)
-    dma = pltpu.SemaphoreType.DMA
     shape = jax.ShapeDtypeStruct
     results = pl.pallas_call(
         functools.partial(kernel, C),
@@ -554,14 +555,6 @@
             pltpu.VMEM((2, 2 * E, H // 2), F32),
             pltpu.VMEM((E, H // 2), F32),
             pltpu.VMEM((2, E, H // 2), F32),
-            dma((half + 1,)),
-            dma((pieces,)),
-            dma((far + 1,)),
-            dma((half,)),
-            dma((C,)),
-            dma((pieces,)),
-            dma((5,)),
-            pltpu.SemaphoreType.REGULAR,
         ],
         compiler_params=pltpu.CompilerParams(
             collective_id=0, has_side_effects=True, vmem_limit_bytes=62208 * 1024
@@ -572,17 +565,19 @@
         out_shape=tuple(shape(r.shape, r.dtype) for r in results),
         in_specs=[hbm] * 6,
         out_specs=tuple([hbm] * 6),
-        scratch_shapes=[dma((6,))],
         compiler_params=pltpu.CompilerParams(vmem_limit_bytes=1024 * 1024),
     )(*results)
 
 
 def deliver(*refs):
-    copies = [pltpu.make_async_copy(refs[i], refs[6 + i], refs[12].at[i]) for i in range(6)]
-    for copy in copies:
-        copy.start()
-    for copy in copies:
-        copy.wait()
+    def run(sem):
+        copies = [pltpu.make_async_copy(refs[i], refs[6 + i], sem.at[i]) for i in range(6)]
+        for copy in copies:
+            copy.start()
+        for copy in copies:
+            copy.wait()
+
+    pl.run_scoped(run, pltpu.SemaphoreType.DMA((6,)))
 
 
 def solution(mesh):

time: 53.3 us -> 52.8 us (level)
  no operation moved by 1% of the time
where the time goes in v4:
time: 52.8 us; the launch traced here: 52.7 us
  Pallas kernels  52.1 us (99%)
  between operations  0.64 us (1%)
    pallas_call x1, Pallas kernels, fused(): pl.pallas_call(functools.partial(kernel, C), out_shape=(pltpu.VMEM((E, T,...  50.4 us
    pallas_call x1, Pallas kernels, fused(): pl.pallas_call(deliver, out_shape=tuple((shape(r.shape, r.dtype) for r in...  1.67 us

profile of v4, /device:TPU:0, one launch (start us, length us, event | category | flops | bytes accessed | tf_op | source)
XLA Modules:
  0.0 52.7 jit_solution(15302895389377882224)
XLA Ops:
  0.6 50.4 %shard_map.109 = (bf16[4,128,1024]{2,1,0:T(8,128)(2,1)S(1)}, bf16[4,128,1024]{2,1,0:T(8,128)(2,1)S(1)}, f32[128,1024]{1,0:T(8,128)S(1)}, f32[4,1024]{1,0:T(4,128...) custom-call(bf16[4,128,1024]{2,1,0:T(8,128)(2,1)} %refs_0_.1, bf16[128,1024]{1,0:T(8,128)(2,1)} %refs_1_.1, ...), custom_call_target="tpu_custom_call" | custom-call | tf_op jit(solution)/shard_map/pallas_call | solution.py:515
  51.0 1.7 %shard_map.110 = (bf16[4,128,1024]{2,1,0:T(8,128)(2,1)}, bf16[4,128,1024]{2,1,0:T(8,128)(2,1)}, f32[128,1024]{1,0:T(8,128)}, f32[4,1024]{1,0:T(4,128)}, f32[4,1024]{1,0:T(4,128)}, /*index=5*/f32[128,1024]{1,0:T(8,128)}) custom-call(bf16[4,128,1024]{2,1,0:T(8,128)(2,1)S(1)} %get-tuple-element.12.refs_0_, bf16[4,128,1024]{2,1,0:T(8,128)(2,1)S(1)} %get-tuple-element.13.refs_1_, ...), custom_call_target="tpu_custom_call" | custom-call | tf_op jit(solution)/shard_map/pallas_call | solution.py:563

commit v5 on v4

--- a/solution.py
+++ b/solution.py
@@ -50,14 +50,14 @@
         functools.partial(work, C, *refs),
         dma((6,)),
         dma((6,)),
-        dma((10,)),
+        dma((12,)),
         dma((half + 1,)),
         dma((2 * far - 1,)),
         dma((far + 1,)),
         dma((half + 1,)),
         dma((C,)),
         dma((2 * far - 1,)),
-        dma((5,)),
+        dma((6,)),
         pltpu.SemaphoreType.REGULAR,
     )
 
@@ -98,7 +98,6 @@
     prv = (m, chip_at(-1) * 2 + c)
     side = (nxt, prv)
     sign = (1, -1)
-    cross = (1 - m, q * 2 + 1 - c)
     beside = (m, f + 2 - 4 * (q % 2))
 
     def along(i):
@@ -123,15 +122,15 @@
     def greet(dev):
         pl.semaphore_signal(barrier, inc=1, device_id=dev, device_id_type=pl.DeviceIdType.MESH)
 
-    lead, deputy = m * (1 - c) == 1, m * c == 1
-    greet((1 - m, q * 2 + m * c))
+    lead, deputy = m * c == 1, m * (1 - c) == 1
+    greet((1 - m, q * 2 + c + (1 - m) * (1 - c)))
 
     @pl.when(jnp.logical_not(lead))
     def _():
         greet(partner)
 
     for ahead in (1, -1):
-        greet((m, chip_at(ahead) * 2 + c + m * (1 - c)))
+        greet((m, chip_at(ahead) * 2 + c * (1 - m)))
 
     def rows_of(core):
         return pl.ds(pl.multiple_of(core * R, R), R)
@@ -144,7 +143,7 @@
     def store(i, src, dst):
         pltpu.make_async_copy(src, dst, st_sem.at[i]).start()
 
-    CX, CXF, AG, PT, PX, PS, RS, AR, SWAP, FIN = range(10)
+    CX, CXF, CXP, AG, PT, PX, PS, RS, AR, SWAP, SWP, FIN = range(12)
 
     ld_inf = load(0, inf_h, inf)
     ld_ctx = load(1, ctx_h, ctx)
@@ -176,6 +175,12 @@
 
     cxf = rc(inf_h, infx, out_sem.at[CXF], cx_rs.at[half], peer)
 
+    cxp = rc(infx, infx, out_sem.at[CXP], cx_rs.at[half], partner)
+
+    def pass_on():
+        cxf.wait_recv()
+        cxp.start()
+
     def sub(core, u):
         return pl.ds(pl.multiple_of(core * R + u * S, S), S)
 
@@ -214,7 +219,7 @@
     def _():
         pl.semaphore_wait(ready, 1)
 
-    cxf.start()
+    pl.when(c == 1)(cxf.start)
     for n in range(half):
         cx(n).start()
 
@@ -359,10 +364,12 @@
             pt_wait(s - 1)
             process([1 - s])
         forward(s, 1)
+        if s == 1:
+            pl.when(c == 1)(pass_on)
         if s > 1:
             process([s - 1])
             if s == 2:
-                cxf.wait_recv()
+                pl.when(c == 0)(cxp.wait_recv)
             scale_in(s - 2)
     scale_in(far - 2)
     both_wait(ag_rs, 2 * (far - 1))
@@ -410,8 +417,8 @@
     to_lines = [ar(1 + i, ars.at[1], along(i)) for i in range(1, lines)]
     from_lines = rc(arr.at[2:], arr.at[2:], out_sem.at[AR], ar_rs.at[2], partner)
     to_other = rc(fin.at[0], fin.at[1], out_sem.at[FIN], ar_rs.at[3], partner)
-    swaps = [rc(swp, swr.at[c], out_sem.at[SWAP], ar_rs.at[4], dev) for dev in (peer, cross)]
-    both_swaps = rc(swr, swr, out_sem.at[SWAP], ar_rs.at[4], peer)
+    swap = rc(swp, swr.at[c], out_sem.at[SWAP], ar_rs.at[4], peer)
+    swap_on = rc(swr.at[c], swr.at[c], out_sem.at[SWP], ar_rs.at[5], partner)
 
     own_half = pl.ds(pl.multiple_of(c * H2, H2), H2)
     other_half = pl.ds(pl.multiple_of((1 - c) * H2, H2), H2)
@@ -434,8 +441,7 @@
             swp[...] = total[E:2 * E]
             fin[0, :E] = total[:E]
             fin[0, E:] = total[2 * E:]
-            for copy in swaps:
-                copy.start()
+            swap.start()
             to_other.start()
 
     def finish(n, members, i):
@@ -484,19 +490,27 @@
     while pending > 1:
         pending -= 1
         finish(pending, every, mine[pending] % half)
+    swap.wait_recv()
+    swap_on.start()
     finish(0, every[:E // 2], mine[0] % half)
     finish(0, every[E // 2:], half)
-    both_swaps.wait_recv()
+    swap_on.wait_recv()
     gi[:, own_half] = fin[0, :E] + swr[c]
     gi[:, other_half] = fin[1, :E] + swr[1 - c]
     store(5, gi, gi_o)
 
     sent = (
-        (CX, cbuf), (CXF, infx), (AG, rsend), (PT, psend), (PX, xrecv),
-        (PS, psend), (RS, rsend), (AR, arr), (SWAP, swr), (FIN, fin.at[0]),
+        (CX, cbuf), (AG, rsend), (PT, psend), (PX, xrecv),
+        (PS, psend), (RS, rsend), (AR, arr), (SWAP, swp), (SWP, swp), (FIN, fin.at[0]),
     )
     for i, ref in sent:
         rc(ref, ref, out_sem.at[i], ar_rs.at[4], peer).wait_send()
+
+    @pl.when(c == 1)
+    def _():
+        cxf.wait_send()
+        cxp.wait_send()
+
     stored = ((hid, hid_o), (gr, gr_o), (gc, gc_o), (gw, gw_o), (go, go_o), (gi, gi_o))
     for i, (src, dst) in enumerate(stored):
         pltpu.make_async_copy(src, dst, st_sem.at[i]).wait()

time: 52.8 us -> 52.4 us (level)
  no operation moved by 1% of the time
where the time goes in v5:
time: 52.4 us; the launch traced here: 52.2 us
  Pallas kernels  51.6 us (98%)
  between operations  0.64 us (1%)
    pallas_call x1, Pallas kernels, fused(): pl.pallas_call(functools.partial(kernel, C), out_shape=(pltpu.VMEM((E, T,...  49.9 us
    pallas_call x1, Pallas kernels, fused(): pl.pallas_call(deliver, out_shape=tuple((shape(r.shape, r.dtype) for r in...  1.67 us

profile of v5, /device:TPU:0, one launch (start us, length us, event | category | flops | bytes accessed | tf_op | source)
XLA Modules:
  0.0 52.2 jit_solution(7378182932950149104)
XLA Ops:
  0.6 49.9 %shard_map.109 = (bf16[4,128,1024]{2,1,0:T(8,128)(2,1)S(1)}, bf16[4,128,1024]{2,1,0:T(8,128)(2,1)S(1)}, f32[128,1024]{1,0:T(8,128)S(1)}, f32[4,1024]{1,0:T(4,128...) custom-call(bf16[4,128,1024]{2,1,0:T(8,128)(2,1)} %refs_0_.1, bf16[128,1024]{1,0:T(8,128)(2,1)} %refs_1_.1, ...), custom_call_target="tpu_custom_call" | custom-call | tf_op jit(solution)/shard_map/pallas_call | solution.py:529
  50.6 1.7 %shard_map.110 = (bf16[4,128,1024]{2,1,0:T(8,128)(2,1)}, bf16[4,128,1024]{2,1,0:T(8,128)(2,1)}, f32[128,1024]{1,0:T(8,128)}, f32[4,1024]{1,0:T(4,128)}, f32[4,1024]{1,0:T(4,128)}, /*index=5*/f32[128,1024]{1,0:T(8,128)}) custom-call(bf16[4,128,1024]{2,1,0:T(8,128)(2,1)S(1)} %get-tuple-element.12.refs_0_, bf16[4,128,1024]{2,1,0:T(8,128)(2,1)S(1)} %get-tuple-element.13.refs_1_, ...), custom_call_target="tpu_custom_call" | custom-call | tf_op jit(solution)/shard_map/pallas_call | solution.py:577

commit v6 on v5

--- a/solution.py
+++ b/solution.py
@@ -50,14 +50,14 @@
         functools.partial(work, C, *refs),
         dma((6,)),
         dma((6,)),
-        dma((12,)),
+        dma((13,)),
         dma((half + 1,)),
         dma((2 * far - 1,)),
         dma((far + 1,)),
         dma((half + 1,)),
         dma((C,)),
         dma((2 * far - 1,)),
-        dma((6,)),
+        dma((7,)),
         pltpu.SemaphoreType.REGULAR,
     )
 
@@ -68,7 +68,7 @@
     hid_o, gc_o, gw_o, gi_o, go_o, gr_o,
     hid, gc, gw, gi, go, gr,
     ctx, cot, res, inf, outf, cbuf, infx, sc, sg, wb, proj, part, xrecv, gall, psend, precv, rsend, rrecv,
-    arb, ars, arr, fin, swp, swr,
+    arb, ars, arr, fin, swp, swr, relay,
     ld_sem, st_sem, out_sem, cx_rs, ag_rs, pt_rs, px_rs, ps_rs, rs_rs, ar_rs, ready,
 ):
     E, T, H = ctx.shape
@@ -143,7 +143,7 @@
     def store(i, src, dst):
         pltpu.make_async_copy(src, dst, st_sem.at[i]).start()
 
-    CX, CXF, CXP, AG, PT, PX, PS, RS, AR, SWAP, SWP, FIN = range(12)
+    CX, CXF, CXP, AG, PT, PX, PS, RS, AR, SWAP, SWP, FIN, RELAY = range(13)
 
     ld_inf = load(0, inf_h, inf)
     ld_ctx = load(1, ctx_h, ctx)
@@ -250,10 +250,16 @@
     for e in range(E):
         sg[e * T:(e + 1) * T, :] = (cot[e].astype(F32) * outw[e:e + 1]).astype(BF16)
 
-    def px(qq, first, last=False):
-        rows = pl.ds(0 if first else E * T // 2, E * T // 2)
+    def px(qq, first, end, last=False):
+        rows = pl.ds(first * T, (end - first) * T)
         i = half if last else qq % half
         return rc(part.at[qq, rows], xrecv.at[qq % half, rows], out_sem.at[PX], px_rs.at[i], peer)
+
+    last_rows = pl.ds((E - 1) * T, T)
+    relay_in = rc(part.at[theirs[0], last_rows], relay, out_sem.at[PX], ar_rs.at[6], partner)
+    relay_out = rc(
+        relay, xrecv.at[theirs[0] % half, last_rows], out_sem.at[RELAY], px_rs.at[half], (1 - m, q * 2)
+    )
 
     def ps(qq):
         return rc(psend.at[qq], precv.at[qq], out_sem.at[PS], ps_rs.at[qq], partner)
@@ -289,13 +295,18 @@
                 sg[...], wb[qq], (((1,), (1,)), ((), ())), preferred_element_type=F32
             ).astype(BF16)
 
-            @pl.when(qq // half != m)
-            def _():
-                px(qq, True).start()
-
             @pl.when(jnp.logical_and(qq // half != m, qq != theirs[0]))
             def _():
-                px(qq, False).start()
+                px(qq, 0, E).start()
+
+            @pl.when(jnp.logical_and(c == 1, qq == theirs[0]))
+            def _():
+                px(qq, 0, E - 1).start()
+
+            @pl.when(jnp.logical_and(c == 0, qq == theirs[0]))
+            def _():
+                px(qq, 0, E - 2).start()
+                relay_in.start()
 
             @pl.when(qq // half == m)
             def _():
@@ -472,7 +483,17 @@
             pending -= 1
             finish(pending, every, mine[pending] % half)
     ar_step(2)
-    px(theirs[0], False, True).start()
+
+    @pl.when(c == 1)
+    def _():
+        relay_in.wait_recv()
+        relay_out.start()
+        px(theirs[0], E - 1, E, True).start()
+
+    @pl.when(c == 0)
+    def _():
+        px(theirs[0], E - 2, E - 1).start()
+
     ps(q).wait_recv()
     for t in range(2):
         both_wait(rs_rs, piece(far - 1, t, 1))
@@ -492,8 +513,8 @@
         finish(pending, every, mine[pending] % half)
     swap.wait_recv()
     swap_on.start()
-    finish(0, every[:E // 2], mine[0] % half)
-    finish(0, every[E // 2:], half)
+    finish(0, every[:E - 1], mine[0] % half)
+    finish(0, every[E - 1:], half)
     swap_on.wait_recv()
     gi[:, own_half] = fin[0, :E] + swr[c]
     gi[:, other_half] = fin[1, :E] + swr[1 - c]
@@ -510,6 +531,7 @@
     def _():
         cxf.wait_send()
         cxp.wait_send()
+        relay_out.wait_send()
 
     stored = ((hid, hid_o), (gr, gr_o), (gc, gc_o), (gw, gw_o), (go, go_o), (gi, gi_o))
     for i, (src, dst) in enumerate(stored):
@@ -569,6 +591,7 @@
             pltpu.VMEM((2, 2 * E, H // 2), F32),
             pltpu.VMEM((E, H // 2), F32),
             pltpu.VMEM((2, E, H // 2), F32),
+            pltpu.VMEM((T, 2 * R), BF16),
         ],
         compiler_params=pltpu.CompilerParams(
             collective_id=0, has_side_effects=True, vmem_limit_bytes=62208 * 1024

time: 52.4 us -> 52.3 us (level)
  no operation moved by 1% of the time
where the time goes in v6:
time: 52.3 us; the launch traced here: 52.2 us
  Pallas kernels  51.5 us (98%)
  between operations  0.64 us (1%)
    pallas_call x1, Pallas kernels, fused(): pl.pallas_call(functools.partial(kernel, C), out_shape=(pltpu.VMEM((E, T,...  49.9 us
    pallas_call x1, Pallas kernels, fused(): pl.pallas_call(deliver, out_shape=tuple((shape(r.shape, r.dtype) for r in...  1.67 us

profile of v6, /device:TPU:0, one launch (start us, length us, event | category | flops | bytes accessed | tf_op | source)
XLA Modules:
  0.0 52.2 jit_solution(12103365554666455271)
XLA Ops:
  0.6 49.9 %shard_map.109 = (bf16[4,128,1024]{2,1,0:T(8,128)(2,1)S(1)}, bf16[4,128,1024]{2,1,0:T(8,128)(2,1)S(1)}, f32[128,1024]{1,0:T(8,128)S(1)}, f32[4,1024]{1,0:T(4,128...) custom-call(bf16[4,128,1024]{2,1,0:T(8,128)(2,1)} %refs_0_.1, bf16[128,1024]{1,0:T(8,128)(2,1)} %refs_1_.1, ...), custom_call_target="tpu_custom_call" | custom-call | tf_op jit(solution)/shard_map/pallas_call | solution.py:551
  50.5 1.7 %shard_map.110 = (bf16[4,128,1024]{2,1,0:T(8,128)(2,1)}, bf16[4,128,1024]{2,1,0:T(8,128)(2,1)}, f32[128,1024]{1,0:T(8,128)}, f32[4,1024]{1,0:T(4,128)}, f32[4,1024]{1,0:T(4,128)}, /*index=5*/f32[128,1024]{1,0:T(8,128)}) custom-call(bf16[4,128,1024]{2,1,0:T(8,128)(2,1)S(1)} %get-tuple-element.12.refs_0_, bf16[4,128,1024]{2,1,0:T(8,128)(2,1)S(1)} %get-tuple-element.13.refs_1_, ...), custom_call_target="tpu_custom_call" | custom-call | tf_op jit(solution)/shard_map/pallas_call | solution.py:600

commit v7 on v6

--- a/solution.py
+++ b/solution.py
@@ -135,15 +135,13 @@
     def rows_of(core):
         return pl.ds(pl.multiple_of(core * R, R), R)
 
-    def load(i, src, dst):
-        copy = pltpu.make_async_copy(src, dst, ld_sem.at[i])
-        copy.start()
-        return copy
-
     def store(i, src, dst):
         pltpu.make_async_copy(src, dst, st_sem.at[i]).start()
 
     CX, CXF, CXP, AG, PT, PX, PS, RS, AR, SWAP, SWP, FIN, RELAY = range(13)
+
+    def load(i, src, dst):
+        return pltpu.make_async_copy(src, dst, ld_sem.at[i])
 
     ld_inf = load(0, inf_h, inf)
     ld_ctx = load(1, ctx_h, ctx)
@@ -151,6 +149,12 @@
     ld_cot = load(3, cot_h, cot)
     ld_w = load(4, w_h, wb.at[q, rows_of(c)])
     ld_res = load(5, res_h, res)
+
+    def load_all():
+        for copy in (ld_inf, ld_ctx, ld_outf, ld_cot, ld_w, ld_res):
+            copy.start()
+
+    pl.when(m == 0)(load_all)
 
     order = [chip_at(-far)] + [chip_at(s * (far - k)) for k in range(1, far) for s in sign] + [q]
 
@@ -222,6 +226,7 @@
     pl.when(c == 1)(cxf.start)
     for n in range(half):
         cx(n).start()
+    pl.when(m != 0)(load_all)
 
     @pl.when(deputy)
     def _():

time: 52.3 us -> 52.3 us (level)
  no operation moved by 1% of the time
where the time goes in v7:
time: 52.3 us; the launch traced here: 52.1 us
  Pallas kernels  51.5 us (98%)
  between operations  0.64 us (1%)
    pallas_call x1, Pallas kernels, fused(): pl.pallas_call(functools.partial(kernel, C), out_shape=(pltpu.VMEM((E, T,...  49.8 us
    pallas_call x1, Pallas kernels, fused(): pl.pallas_call(deliver, out_shape=tuple((shape(r.shape, r.dtype) for r in...  1.67 us

profile of v7, /device:TPU:0, one launch (start us, length us, event | category | flops | bytes accessed | tf_op | source)
XLA Modules:
  0.0 52.1 jit_solution(6400261746898995424)
XLA Ops:
  0.6 49.8 %shard_map.109 = (bf16[4,128,1024]{2,1,0:T(8,128)(2,1)S(1)}, bf16[4,128,1024]{2,1,0:T(8,128)(2,1)S(1)}, f32[128,1024]{1,0:T(8,128)S(1)}, f32[4,1024]{1,0:T(4,128...) custom-call(bf16[4,128,1024]{2,1,0:T(8,128)(2,1)} %refs_0_.1, bf16[128,1024]{1,0:T(8,128)(2,1)} %refs_1_.1, ...), custom_call_target="tpu_custom_call" | custom-call | tf_op jit(solution)/shard_map/pallas_call | solution.py:556
  50.5 1.7 %shard_map.110 = (bf16[4,128,1024]{2,1,0:T(8,128)(2,1)}, bf16[4,128,1024]{2,1,0:T(8,128)(2,1)}, f32[128,1024]{1,0:T(8,128)}, f32[4,1024]{1,0:T(4,128)}, f32[4,1024]{1,0:T(4,128)}, /*index=5*/f32[128,1024]{1,0:T(8,128)}) custom-call(bf16[4,128,1024]{2,1,0:T(8,128)(2,1)S(1)} %get-tuple-element.12.refs_0_, bf16[4,128,1024]{2,1,0:T(8,128)(2,1)S(1)} %get-tuple-element.13.refs_1_, ...), custom_call_target="tpu_custom_call" | custom-call | tf_op jit(solution)/shard_map/pallas_call | solution.py:605
